TPU v7x, 32 devices: a whole 2x2x4 slice. The times are simulated.
32 devices in a mesh: gx: 2 (over x), gy: 4 (over z), lev: 4 (over y, core).
Axes of the slice: x: 2, y: 2, z: 4, core: 2. Of those that a mesh axis runs over, the one named last changes fastest.
Arguments:
- zonal: float32 [128, 64, 512], P('lev', 'gx', 'gy'), may hold values from -6 to 6
- meridional: float32 [128, 64, 512], P('lev', 'gx', 'gy'), may hold values from -6 to 6
- vertical: float32 [128, 64, 512], P('lev', 'gx', 'gy'), may hold values from -4 to 4
- pressure: float32 [128, 64, 512], P('lev', 'gx', 'gy'), may hold values from -6 to 6
- coupling: float32 [128, 64, 512], P('lev', 'gx', 'gy'), may hold values from 0.125 to 32768
- surface: int32 [64, 512], P('gx', 'gy'), may hold values from 0 to 16
- lid_flag: int32 [64, 512], P('gx', 'gy'), may hold values from 0 to 1
Outputs:
- zonal_out: float32 [128, 64, 512], P('lev', 'gx', 'gy')
- meridional_out: float32 [128, 64, 512], P('lev', 'gx', 'gy')
- vertical_out: float32 [128, 64, 512], P('lev', 'gx', 'gy')
- pressure_out: float32 [128, 64, 512], P('lev', 'gx', 'gy')
Inputs may be any that keep to these rules, and one draw needn't show every extreme that they name: `surface`: the number of lowest levels of a column that lie below the terrain. `lid_flag`: 1 closes the column's top with a rigid lid, 0 leaves it open.
All inputs are finite; a program needn't handle non-finite values.
Results may differ from a plain program's by a relative error of at most 0.0003.
Values sent between devices are 32-bit elements; how exact they have to be, the bound alone decides.
No kernel may reach another device: no remote copies, remote signals or barrier semaphores. Data moves between devices by JAX's collectives and lax.ppermute only.
A program may use at most 128 MiB of HBM per device.

v0:
```python
import functools

import jax
import jax.numpy as jnp
from jax import lax
from jax.experimental import pallas as pl
from jax.experimental.pallas import tpu as pltpu
from jax.sharding import PartitionSpec as P

SUBSTEPS = 3
H_STEP = 0.25
D_STEP = 0.25
V_STEP = 0.5
P_STEP = 0.5
F32 = jnp.float32
PAD = 8

VMEM = pl.BlockSpec(memory_space=pltpu.VMEM)
SMEM = pl.BlockSpec(memory_space=pltpu.SMEM)


def call(kernel, outs, args, scratch=(), smem=0):
    specs = [SMEM] * smem + [VMEM] * (len(args) - smem)
    return pl.pallas_call(
        kernel,
        out_shape=[jax.ShapeDtypeStruct(s, F32) for s in outs],
        in_specs=specs,
        out_specs=[VMEM] * len(outs),
        scratch_shapes=list(scratch),
        compiler_params=pltpu.CompilerParams(vmem_limit_bytes=20 * 1024 * 1024),
    )(*args)


def sides(n):
    return 1 if n <= 2 else 2


def views(refs, rows):
    if len(refs) == 1:
        up = [refs[0].at[r] for r in range(rows)]
        down = [refs[0].at[rows + r] for r in range(rows)]
    else:
        up = [refs[0].at[r] for r in range(rows)]
        down = [refs[1].at[r] for r in range(rows)]
    return up, down


def message_shapes(n, rows, plane):
    if sides(n) == 1:
        return [(2 * rows,) + plane]
    return [(rows,) + plane] * 2


def exchange(messages, axis):
    n = lax.axis_size(axis)
    if n == 1:
        return messages
    up = [(i, (i + 1) % n) for i in range(n)]
    if n == 2:
        return [lax.ppermute(messages[0], axis, up)]
    down = [(j, i) for i, j in up]
    return [lax.ppermute(messages[0], axis, up), lax.ppermute(messages[1], axis, down)]


def source_of(group, m, n):
    return group ^ m if n & (n - 1) == 0 else (group - m) % n


def gather_lev(message):
    n = lax.axis_size("lev")
    got = []
    for m in range(1, n):
        if n & (n - 1) == 0:
            pairs = [(i, i ^ m) for i in range(n)]
        else:
            pairs = [(i, (i + m) % n) for i in range(n)]
        got.append(lax.ppermute(message, "lev", pairs))
    return got


def pack_columns(ref, picks, outs):
    depth, ni, nj = ref.shape
    per = nj // ni
    for b in range(depth // per):
        block = ref[b * per : (b + 1) * per].reshape(per * ni, nj)
        turned = block.T
        for c, out in zip(picks, outs):
            out[b : b + 1, :] = turned[c : c + 1, :]


def send_rows(ref, out_up, out_down, wide):
    ni = ref.shape[1]
    for r in range(wide):
        out_up[r][...] = ref[:, ni - wide + r, :]
        out_down[r][...] = ref[:, r, :]


def first_kernel(sx, sy, zonal, merid, press, *outs):
    mx, my = outs[:sx], outs[sx : sx + sy]
    nj = press.shape[2]
    xu, xd = views(mx, 3)
    send_rows(press, xu[:2], xd[:2], 2)
    send_rows(zonal, xu[2:], xd[2:], 1)
    yu, yd = views(my, 3)
    pack_columns(press, (nj - 2, nj - 1, 0, 1), (yu[0], yu[1], yd[0], yd[1]))
    pack_columns(merid, (nj - 1, 0), (yu[2], yd[2]))


def factor_kernel(groups, group_ref, c, surface, lid, inv, mul, g0, gl, planes):
    depth, ni, nj = c.shape
    last, half = depth - 1, depth // 2
    group = group_ref[0]
    bottom = group == 0
    top = group == groups - 1
    ground = surface[...] - group * depth
    lidf = jnp.where(top, lid[...].astype(F32), 0.0)
    zero = jnp.zeros((ni, nj), F32)

    def coupling(k):
        return jnp.where(ground <= k - 1, c[k], 0.0)

    def diag(k):
        low = c[k] if k > 0 else jnp.where(bottom, c[k], 0.0)
        high = c[k + 1] if k < last else lidf * c[k]
        return 1.0 + low + high

    lo, hi = None, None
    for s in range(half):
        k, j = s, last - s
        d_lo, d_hi = diag(k), diag(j)
        if s:
            e_lo = coupling(k)
            m_lo = e_lo * lo
            mul[k] = m_lo
            d_lo = d_lo - e_lo * m_lo
            e_hi = coupling(j + 1)
            m_hi = e_hi * hi
            mul[j + 1] = m_hi
            d_hi = d_hi - e_hi * m_hi
        if j == half:
            e_mid = coupling(half)
            lo = jnp.where(ground <= k, 1.0 / d_lo, 0.0)
            m_mid = e_mid * lo
            mul[half] = m_mid
            d_hi = d_hi - e_mid * m_mid
        else:
            lo = jnp.where(ground <= k, 1.0 / d_lo, 0.0)
        hi = jnp.where(ground <= j, 1.0 / d_hi, 0.0)
        inv[k] = lo
        inv[j] = hi
    one = jnp.ones((ni, nj), F32)
    t0 = [one] + [None] * (half - 1)
    tl = [one] + [None] * (half - 1)
    for s in range(1, half):
        t0[s] = mul[s] * t0[s - 1]
        tl[s] = mul[last - s + 1] * tl[s - 1]
        g0[s] = t0[s]
        gl[last - s] = tl[s]
    g0[0] = one
    gl[last] = one
    xh0 = inv[half] * (mul[half] * t0[half - 1])
    xhl = inv[half] * tl[half - 1]
    xk0 = inv[half - 1] * t0[half - 1] + mul[half] * xh0
    xkl = mul[half] * xhl
    g0[half], gl[half] = xh0, xhl
    g0[half - 1], gl[half - 1] = xk0, xkl
    for s in range(1, half):
        k, j = half - 1 - s, half + s
        xk0 = inv[k] * g0[k] + mul[k + 1] * xk0
        xkl = mul[k + 1] * xkl
        xh0 = mul[j] * xh0
        xhl = inv[j] * gl[j] + mul[j] * xhl
        g0[k], gl[k] = xk0, xkl
        g0[j], gl[j] = xh0, xhl
    planes[0] = g0[0]
    planes[1] = g0[last]
    planes[2] = gl[last]
    planes[3] = c[0]


def advance_kernel(first, sx, sy, *refs):
    refs = list(refs)
    take = lambda n: [refs.pop(0) for _ in range(n)]
    zonal, merid, vert, press, inv, mul = take(6)
    ox, oy = take(sx), take(sy)
    rx, ry = take(sx), take(sy)
    uh, vh = (None, None) if first else take(2)
    zonal_out, merid_out, y_out, part, planes, uh_out, vh_out = take(7)
    pe, ue, tt, tsq = take(4)
    depth, ni, nj = press.shape
    last, half, per = depth - 1, depth // 2, nj // ni
    wide = 3 if first else 2
    oxu, oxd = views(ox, wide)
    rlo, rhi = views(rx, wide)
    oyu, oyd = views(oy, wide)
    clo, chi = views(ry, wide)

    u_lo = rlo[2][...] if first else uh[0]
    u_hi = rhi[2][...] if first else uh[1]
    u_lo = u_lo - H_STEP * (oxd[0][...] - rlo[0][...])
    u_hi = u_hi - H_STEP * (rhi[1][...] - oxu[1][...])
    uh_out[0], uh_out[1] = u_lo, u_hi
    v_lo = clo[2][...] if first else vh[0]
    v_hi = chi[2][...] if first else vh[1]
    v_lo = v_lo - H_STEP * (oyd[0][...] - clo[0][...])
    v_hi = v_hi - H_STEP * (chi[1][...] - oyu[1][...])
    vh_out[0], vh_out[1] = v_lo, v_hi

    ue[:, PAD - 1, :] = u_lo
    ue[:, PAD + ni, :] = u_hi
    pe[:, PAD - 1, :] = rlo[1][...]
    pe[:, PAD + ni, :] = rhi[0][...]
    p_lo, p_hi = clo[1][...], chi[0][...]
    tsq[...] = jnp.zeros((nj, nj), F32)
    mid = nj // 2
    for b in range(depth // per):
        tsq[0:1, :] = p_hi[b : b + 1]
        tsq[nj - 1 : nj, :] = p_lo[b : b + 1]
        tsq[mid : mid + 1, :] = v_hi[b : b + 1]
        tsq[mid - 1 : mid, :] = v_lo[b : b + 1]
        tt[b * per : (b + 1) * per] = tsq[...].T.reshape(per, ni, nj)

    def copy(k, _):
        pe[k, PAD : PAD + ni, :] = press[k]
        return _

    lax.fori_loop(0, depth, copy, 0, unroll=4)
    lane = lax.broadcasted_iota(jnp.int32, (ni, nj), 1)
    at_first, at_last = lane == 0, lane == nj - 1

    def stencil(k, _):
        p, t = press[k], tt[k]
        u = zonal[k] - H_STEP * (pe[k, PAD + 1 : PAD + 1 + ni, :] - pe[k, PAD - 1 : PAD - 1 + ni, :])
        zonal_out[k] = u
        ue[k, PAD : PAD + ni, :] = u
        right = pltpu.roll(jnp.where(at_first, t, p), nj - 1, 1)
        left = pltpu.roll(jnp.where(at_last, t, p), 1, 1)
        v = merid[k] - H_STEP * (right - left)
        merid_out[k] = v
        t = pltpu.roll(t, mid, 1)
        right = pltpu.roll(jnp.where(at_first, t, v), nj - 1, 1)
        left = pltpu.roll(jnp.where(at_last, t, v), 1, 1)
        spread = (ue[k, PAD + 1 : PAD + 1 + ni, :] - ue[k, PAD - 1 : PAD - 1 + ni, :]) + (right - left)
        part[k] = p - D_STEP * spread
        return _

    lax.fori_loop(0, depth, stencil, 0, unroll=2)

    lo = vert[0] - V_STEP * part[1]
    hi = vert[last] + V_STEP * part[last - 1]
    y_out[0], y_out[last] = lo, hi
    for s in range(1, half):
        k, j = s, last - s
        lo = (vert[k] - V_STEP * (part[k + 1] - part[k - 1])) + mul[k] * lo
        hi = (vert[j] - V_STEP * (part[j + 1] - part[j - 1])) + mul[j + 1] * hi
        y_out[k], y_out[j] = lo, hi
    hi = inv[half] * (hi + mul[half] * lo)
    lo = inv[half - 1] * lo + mul[half] * hi
    y_out[half], y_out[half - 1] = hi, lo
    for s in range(1, half):
        k, j = half - 1 - s, half + s
        lo = inv[k] * y_out[k] + mul[k + 1] * lo
        hi = inv[j] * y_out[j] + mul[j] * hi
        y_out[k], y_out[j] = lo, hi
    planes[0], planes[1] = lo, hi
    planes[2], planes[3] = part[0], part[last]


def finish_kernel(groups, final, sx, sy, group_ref, *refs):
    refs = list(refs)
    take = lambda n: [refs.pop(0) for _ in range(n)]
    y, part, g0, gl = take(4)
    own_s, own_l = take(2)
    got_s, got_l = take(groups - 1), take(groups - 1)
    vert_out, press_out = take(2)
    mx, my = ([], []) if final else (take(sx), take(sy))
    st, lv = take(2)
    depth, ni, nj = y.shape
    group = group_ref[0]
    st[group] = own_s[...]
    lv[group] = own_l[...]
    for m in range(1, groups):
        src = source_of(group, m, groups)
        st[src] = got_s[m - 1][...]
        lv[src] = got_l[m - 1][...]
    zero = jnp.zeros((ni, nj), F32)
    z_top, z_bot = [], []
    for g in range(groups):
        below = V_STEP * lv[g - 1, 3] if g else zero
        above = V_STEP * lv[g + 1, 2] if g < groups - 1 else zero
        z_top.append(lv[g, 0] + st[g, 0] * below - st[g, 1] * above)
        z_bot.append(lv[g, 1] + st[g, 1] * below - st[g, 2] * above)
    ratios, parts = [zero], [zero]
    for g in range(1, groups):
        cg = st[g, 3]
        down = cg * st[g - 1, 1]
        pivot = 1.0 / (1.0 + cg * (st[g - 1, 2] + st[g, 0]) - down * ratios[-1])
        parts.append((cg * (z_bot[g - 1] - z_top[g]) + down * parts[-1]) * pivot)
        ratios.append(cg * st[g, 1] * pivot)
    flux = [zero] * (groups + 1)
    for g in range(groups - 1, 0, -1):
        flux[g] = parts[g] + ratios[g] * flux[g + 1]
    alpha, beta, under = zero, zero, zero
    for g in range(groups):
        mine = group == g
        if g:
            alpha = jnp.where(mine, V_STEP * lv[g - 1, 3] + flux[g], alpha)
            bot = z_bot[g - 1] + st[g - 1, 1] * flux[g - 1] - st[g - 1, 2] * flux[g]
            under = jnp.where(mine, bot, under)
        if g < groups - 1:
            beta = jnp.where(mine, -(V_STEP * lv[g + 1, 2] + flux[g + 1]), beta)

    def level(k, w_prev):
        w = y[k] + g0[k] * alpha + gl[k] * beta
        vert_out[k] = w
        press_out[k] = part[k] - P_STEP * (w - w_prev)
        return w

    lax.fori_loop(0, depth, level, under, unroll=4)
    if not final:
        xu, xd = views(mx, 2)
        send_rows(press_out, xu, xd, 2)
        yu, yd = views(my, 2)
        pack_columns(press_out, (nj - 2, nj - 1, 0, 1), (yu[0], yu[1], yd[0], yd[1]))


def body(zonal, meridional, vertical, pressure, coupling, surface, lid_flag):
    depth, ni, nj = coupling.shape
    full = (depth, ni, nj)
    groups = lax.axis_size("lev")
    group = lax.axis_index("lev").astype(jnp.int32)[None]
    nx, ny = lax.axis_size("gx"), lax.axis_size("gy")
    sx, sy = sides(nx), sides(ny)
    per = nj // ni
    row, col = (depth, nj), (depth // per, nj)

    messages = list(
        call(
            functools.partial(first_kernel, sx, sy),
            message_shapes(nx, 3, row) + message_shapes(ny, 3, col),
            (zonal, meridional, pressure),
        )
    )
    ox, oy = messages[:sx], messages[sx:]
    rx, ry = exchange(ox, "gx"), exchange(oy, "gy")
    inv, mul, g0, gl, own_s = call(
        functools.partial(factor_kernel, groups),
        [full] * 4 + [(4, ni, nj)],
        (group, coupling, surface, lid_flag),
        smem=1,
    )
    got_s = gather_lev(own_s)
    uh = vh = None
    for substep in range(SUBSTEPS):
        first, final = substep == 0, substep == SUBSTEPS - 1
        args = [zonal, meridional, vertical, pressure, inv, mul] + ox + oy + rx + ry
        if not first:
            args += [uh, vh]
        zonal, meridional, y, part, own_l, uh, vh = call(
            functools.partial(advance_kernel, first, sx, sy),
            [full] * 4 + [(4, ni, nj), (2,) + row, (2,) + col],
            args,
            scratch=[
                pltpu.VMEM((depth, ni + 2 * PAD, nj), F32),
                pltpu.VMEM((depth, ni + 2 * PAD, nj), F32),
                pltpu.VMEM(full, F32),
                pltpu.VMEM((nj, nj), F32),
            ],
        )
        got_l = gather_lev(own_l)
        outs = [full, full]
        if not final:
            outs += message_shapes(nx, 2, row) + message_shapes(ny, 2, col)
        results = call(
            functools.partial(finish_kernel, groups, final, sx, sy),
            outs,
            [group, y, part, g0, gl, own_s, own_l] + got_s + got_l,
            scratch=[pltpu.VMEM((groups, 4, ni, nj), F32)] * 2,
            smem=1,
        )
        vertical, pressure = results[:2]
        if not final:
            ox, oy = list(results[2 : 2 + sx]), list(results[2 + sx :])
            rx, ry = exchange(ox, "gx"), exchange(oy, "gy")
    return (zonal, meridional, vertical, pressure)


def solution(mesh):
    block = P("lev", "gx", "gy")
    plane = P("gx", "gy")
    return jax.shard_map(
        body,
        mesh=mesh,
        in_specs=(block,) * 5 + (plane,) * 2,
        out_specs=(block,) * 4,
        check_vma=False,
    )
```

profile of v0, /device:TPU:0, one launch (start us, length us, event | category | flops | bytes accessed | tf_op | source)
XLA Modules:
  0.0 58.7 jit_solution(3696633276442188754)
XLA Ops:
  0.6 0.0 copy-start
  0.6 1.0 %copy-done = f32[32,32,128]{2,1,0:T(8,128)S(1)} copy-done((f32[32,32,128]{2,1,0:T(8,128)S(1)}, f32[32,32,128]{2,1,0:T(8,128)}, u32[]{:S(2)}) %copy-start) | copy-done | bytes 524312
  1.7 1.0 %copy-done.2 = f32[32,32,128]{2,1,0:T(8,128)S(1)} copy-done((f32[32,32,128]{2,1,0:T(8,128)S(1)}, f32[32,32,128]{2,1,0:T(8,128)}, u32[]{:S(2)}) %copy-start.2) | copy-done | bytes 524312
  2.7 1.0 %copy-done.4 = f32[32,32,128]{2,1,0:T(8,128)S(1)} copy-done((f32[32,32,128]{2,1,0:T(8,128)S(1)}, f32[32,32,128]{2,1,0:T(8,128)}, u32[]{:S(2)}) %copy-start.4) | copy-done | bytes 524312
  3.8 0.3 shard_map.103
  4.1 0.0 copy-start.1
  4.1 3.0 %collective-permute-start = (f32[6,32,128]{2,1,0:T(8,128)S(1)}, f32[6,32,128]{2,1,0:T(8,128)S(1)}, u32[]{:S(2)}, u32[]{:S(2)}) collective-permute-start(f32[6,32,128]{2,1,0:T(8,128)S(1)} %get-tuple-element.45.refs_6_), channel_id=1, source_target_pairs={{0,16},{16,0},{1,17},{17,1},{2,18},{18,2},{3,19},{19,3},{4,20},{20... | collective-permute-start | bytes 294920 | tf_op jit(solution)/shard_map/ppermute | solution.py:60
  7.1 1.0 %copy-done.7 = f32[32,32,128]{2,1,0:T(8,128)S(1)} copy-done((f32[32,32,128]{2,1,0:T(8,128)S(1)}, f32[32,32,128]{2,1,0:T(8,128)}, u32[]{:S(2)}) %copy-start.7) | copy-done | bytes 524312
  8.2 0.7 %copy-done.8 = s32[32,128]{1,0:T(8,128)S(1)} copy-done((s32[32,128]{1,0:T(8,128)S(1)}, s32[32,128]{1,0:T(8,128)}, u32[]{:S(2)}) %copy-start.8) | copy-done | bytes 16408
  8.9 0.7 %copy-done.9 = s32[32,128]{1,0:T(8,128)S(1)} copy-done((s32[32,128]{1,0:T(8,128)S(1)}, s32[32,128]{1,0:T(8,128)}, u32[]{:S(2)}) %copy-start.9) | copy-done | bytes 16408
  9.6 0.3 shard_map.102
  9.9 0.7 %collective-permute-start.5 = (f32[4,32,128]{2,1,0:T(8,128)S(1)}, f32[4,32,128]{2,1,0:T(8,128)S(1)}, u32[]{:S(2)}, u32[]{:S(2)}) collective-permute-start(f32[4,32,128]{2,1,0:T(8,128)S(1)} %get-tuple-element.54.refs_4_), channel_id=1, source_target_pairs={{0,3},{1,2},{2,1},{3,0},{4,7},{5,6},{6,5},{7,4},{8,11},{9,10},{10,... | collective-permute-start | bytes 196616 | tf_op jit(solution)/shard_map/ppermute | solution.py:77
  10.6 1.6 %collective-permute-start.1 = (f32[3,8,128]{2,1,0:T(8,128)S(1)}, f32[3,8,128]{2,1,0:T(8,128)S(1)}, u32[]{:S(2)}, u32[]{:S(2)}) collective-permute-start(f32[3,8,128]{2,1,0:T(8,128)S(1)} %get-tuple-element.46.refs_7_), channel_id=1, source_target_pairs={{0,4},{4,8},{8,12},{12,0},{1,5},{5,9},{9,13},{13,1},{2,6},{6,10},{... | collective-permute-start | bytes 36872 | tf_op jit(solution)/shard_map/ppermute | solution.py:62
  12.2 2.2 %collective-permute-start.2 = (f32[3,8,128]{2,1,0:T(8,128)S(1)}, f32[3,8,128]{2,1,0:T(8,128)S(1)}, u32[]{:S(2)}, u32[]{:S(2)}) collective-permute-start(f32[3,8,128]{2,1,0:T(8,128)S(1)} %get-tuple-element.47.refs_8_), channel_id=1, source_target_pairs={{4,0},{8,4},{12,8},{0,12},{5,1},{9,5},{13,9},{1,13},{6,2},{10,6},{... | collective-permute-start | bytes 36872 | tf_op jit(solution)/shard_map/ppermute | solution.py:62
  14.5 0.9 %collective-permute-start.4 = (f32[4,32,128]{2,1,0:T(8,128)S(1)}, f32[4,32,128]{2,1,0:T(8,128)S(1)}, u32[]{:S(2)}, u32[]{:S(2)}) collective-permute-start(f32[4,32,128]{2,1,0:T(8,128)S(1)} %get-tuple-element.54.refs_4_), channel_id=1, source_target_pairs={{0,2},{1,3},{2,0},{3,1},{4,6},{5,7},{6,4},{7,5},{8,10},{9,11},{10,... | collective-permute-start | bytes 196616 | tf_op jit(solution)/shard_map/ppermute | solution.py:77
  15.4 0.8 %collective-permute-done.1.refs_10_ = f32[3,8,128]{2,1,0:T(8,128)S(1)} collective-permute-done((f32[3,8,128]{2,1,0:T(8,128)S(1)}, f32[3,8,128]{2,1,0:T(8,128)S(1)}, u32[]{:S(2)}, u32[]{:S(2)}) %collective-permute-start.1) | collective-permute-done | bytes 12320 | tf_op jit(solution)/shard_map/ppermute | solution.py:62
  16.2 0.1 collective-permute-start.3
  16.3 0.0 collective-permute-done.2.refs_11_
  16.3 0.0 collective-permute-done.refs_9_
  16.4 3.3 %shard_map.104 = (f32[32,32,128]{2,1,0:T(8,128)S(1)}, f32[32,32,128]{2,1,0:T(8,128)S(1)}, f32[32,32,128]{2,1,0:T(8,128)S(1)}, f32[32,32,128]{2,1,0:T(8,128)S(1)}...) custom-call(f32[32,32,128]{2,1,0:T(8,128)S(1)} %copy-done.1, ...), custom_call_target="tpu_custom_call" | custom-call | tf_op jit(solution)/shard_map/pallas_call | solution.py:24
  19.7 0.9 %collective-permute-start.8 = (f32[4,32,128]{2,1,0:T(8,128)S(1)}, f32[4,32,128]{2,1,0:T(8,128)S(1)}, u32[]{:S(2)}, u32[]{:S(2)}) collective-permute-start(f32[4,32,128]{2,1,0:T(8,128)S(1)} %get-tuple-element.55.refs_5_), channel_id=1, source_target_pairs={{0,3},{1,2},{2,1},{3,0},{4,7},{5,6},{6,5},{7,4},{8,11},{9,10},{10,... | collective-permute-start | bytes 196616 | tf_op jit(solution)/shard_map/ppermute | solution.py:77
  20.6 1.2 %collective-permute-start.7 = (f32[4,32,128]{2,1,0:T(8,128)S(1)}, f32[4,32,128]{2,1,0:T(8,128)S(1)}, u32[]{:S(2)}, u32[]{:S(2)}) collective-permute-start(f32[4,32,128]{2,1,0:T(8,128)S(1)} %get-tuple-element.55.refs_5_), channel_id=1, source_target_pairs={{0,2},{1,3},{2,0},{3,1},{4,6},{5,7},{6,4},{7,5},{8,10},{9,11},{10,... | collective-permute-start | bytes 196616 | tf_op jit(solution)/shard_map/ppermute | solution.py:77
  21.8 0.0 collective-permute-done.5.refs_8_
  21.8 0.0 collective-permute-start.6
  21.8 1.8 %collective-permute-done.8.refs_11_ = f32[4,32,128]{2,1,0:T(8,128)S(1)} collective-permute-done((f32[4,32,128]{2,1,0:T(8,128)S(1)}, f32[4,32,128]{2,1,0:T(8,128)S(1)}, u32[]{:S(2)}, u32[]{:S(2)}) %collective-permute-start.8) | collective-permute-done | bytes 65568 | tf_op jit(solution)/shard_map/ppermute | solution.py:77
  23.6 2.0 %collective-permute-done.7.refs_10_ = f32[4,32,128]{2,1,0:T(8,128)S(1)} collective-permute-done((f32[4,32,128]{2,1,0:T(8,128)S(1)}, f32[4,32,128]{2,1,0:T(8,128)S(1)}, u32[]{:S(2)}, u32[]{:S(2)}) %collective-permute-start.7) | collective-permute-done | bytes 65568 | tf_op jit(solution)/shard_map/ppermute | solution.py:77
  25.6 0.5 shard_map.105
  26.1 0.6 %collective-permute-start.9 = (f32[4,32,128]{2,1,0:T(8,128)S(1)}, f32[4,32,128]{2,1,0:T(8,128)S(1)}, u32[]{:S(2)}, u32[]{:S(2)}) collective-permute-start(f32[4,32,128]{2,1,0:T(8,128)S(1)} %get-tuple-element.58.refs_6_), channel_id=1, source_target_pairs={{0,16},{16,0},{1,17},{17,1},{2,18},{18,2},{3,19},{19,3},{4,20},{20... | collective-permute-start | bytes 196616 | tf_op jit(solution)/shard_map/ppermute | solution.py:60
  26.7 0.6 collective-permute-start.10
  27.2 3.3 %collective-permute-start.11 = (f32[2,8,128]{2,1,0:T(8,128)S(1)}, f32[2,8,128]{2,1,0:T(8,128)S(1)}, u32[]{:S(2)}, u32[]{:S(2)}) collective-permute-start(f32[2,8,128]{2,1,0:T(8,128)S(1)} %get-tuple-element.60.refs_8_), channel_id=1, source_target_pairs={{4,0},{8,4},{12,8},{0,12},{5,1},{9,5},{13,9},{1,13},{6,2},{10,6},{... | collective-permute-start | bytes 24584 | tf_op jit(solution)/shard_map/ppermute | solution.py:62
  30.5 1.6 %collective-permute-done.10.refs_10_ = f32[2,8,128]{2,1,0:T(8,128)S(1)} collective-permute-done((f32[2,8,128]{2,1,0:T(8,128)S(1)}, f32[2,8,128]{2,1,0:T(8,128)S(1)}, u32[]{:S(2)}, u32[]{:S(2)}) %collective-permute-start.10) | collective-permute-done | bytes 8224 | tf_op jit(solution)/shard_map/ppermute | solution.py:62
  32.1 3.3 %shard_map.106 = (f32[32,32,128]{2,1,0:T(8,128)S(1)}, f32[32,32,128]{2,1,0:T(8,128)S(1)}, f32[32,32,128]{2,1,0:T(8,128)S(1)}, f32[32,32,128]{2,1,0:T(8,128)S(1)}...) custom-call(f32[32,32,128]{2,1,0:T(8,128)S(1)} %get-tuple-element.48.refs_0_, ...), custom_call_target="tpu_custom_call" | custom-call | tf_op jit(solution)/shard_map/pallas_call | solution.py:24
  35.5 0.1 collective-permute-start.14
  35.6 0.8 %collective-permute-start.13 = (f32[4,32,128]{2,1,0:T(8,128)S(1)}, f32[4,32,128]{2,1,0:T(8,128)S(1)}, u32[]{:S(2)}, u32[]{:S(2)}) collective-permute-start(f32[4,32,128]{2,1,0:T(8,128)S(1)} %get-tuple-element.67.refs_5_), channel_id=1, source_target_pairs={{0,2},{1,3},{2,0},{3,1},{4,6},{5,7},{6,4},{7,5},{8,10},{9,11},{10,... | collective-permute-start | bytes 196616 | tf_op jit(solution)/shard_map/ppermute | solution.py:77
  36.3 1.1 %collective-permute-start.12 = (f32[4,32,128]{2,1,0:T(8,128)S(1)}, f32[4,32,128]{2,1,0:T(8,128)S(1)}, u32[]{:S(2)}, u32[]{:S(2)}) collective-permute-start(f32[4,32,128]{2,1,0:T(8,128)S(1)} %get-tuple-element.67.refs_5_), channel_id=1, source_target_pairs={{0,1},{1,0},{2,3},{3,2},{4,5},{5,4},{6,7},{7,6},{8,9},{9,8},{10,11... | collective-permute-start | bytes 196616 | tf_op jit(solution)/shard_map/ppermute | solution.py:77
  37.4 1.9 %collective-permute-done.14.refs_11_ = f32[4,32,128]{2,1,0:T(8,128)S(1)} collective-permute-done((f32[4,32,128]{2,1,0:T(8,128)S(1)}, f32[4,32,128]{2,1,0:T(8,128)S(1)}, u32[]{:S(2)}, u32[]{:S(2)}) %collective-permute-start.14) | collective-permute-done | bytes 65568 | tf_op jit(solution)/shard_map/ppermute | solution.py:77
  39.3 1.3 %collective-permute-done.13.refs_10_ = f32[4,32,128]{2,1,0:T(8,128)S(1)} collective-permute-done((f32[4,32,128]{2,1,0:T(8,128)S(1)}, f32[4,32,128]{2,1,0:T(8,128)S(1)}, u32[]{:S(2)}, u32[]{:S(2)}) %collective-permute-start.13) | collective-permute-done | bytes 65568 | tf_op jit(solution)/shard_map/ppermute | solution.py:77
  40.6 0.5 shard_map.107
  41.1 1.6 %collective-permute-start.15 = (f32[4,32,128]{2,1,0:T(8,128)S(1)}, f32[4,32,128]{2,1,0:T(8,128)S(1)}, u32[]{:S(2)}, u32[]{:S(2)}) collective-permute-start(f32[4,32,128]{2,1,0:T(8,128)S(1)} %get-tuple-element.70.refs_6_), channel_id=1, source_target_pairs={{0,16},{16,0},{1,17},{17,1},{2,18},{18,2},{3,19},{19,3},{4,20},{20... | collective-permute-start | bytes 196616 | tf_op jit(solution)/shard_map/ppermute | solution.py:60
  42.6 0.4 collective-permute-start.16
  43.1 3.4 %collective-permute-start.17 = (f32[2,8,128]{2,1,0:T(8,128)S(1)}, f32[2,8,128]{2,1,0:T(8,128)S(1)}, u32[]{:S(2)}, u32[]{:S(2)}) collective-permute-start(f32[2,8,128]{2,1,0:T(8,128)S(1)} %get-tuple-element.72.refs_8_), channel_id=1, source_target_pairs={{4,0},{8,4},{12,8},{0,12},{5,1},{9,5},{13,9},{1,13},{6,2},{10,6},{... | collective-permute-start | bytes 24584 | tf_op jit(solution)/shard_map/ppermute | solution.py:62
  46.5 1.6 %collective-permute-done.16.refs_10_ = f32[2,8,128]{2,1,0:T(8,128)S(1)} collective-permute-done((f32[2,8,128]{2,1,0:T(8,128)S(1)}, f32[2,8,128]{2,1,0:T(8,128)S(1)}, u32[]{:S(2)}, u32[]{:S(2)}) %collective-permute-start.16) | collective-permute-done | bytes 8224 | tf_op jit(solution)/shard_map/ppermute | solution.py:62
  48.1 4.1 %shard_map.108 = (f32[32,32,128]{2,1,0:T(8,128)}, f32[32,32,128]{2,1,0:T(8,128)}, f32[32,32,128]{2,1,0:T(8,128)S(1)}, f32[32,32,128]{2,1,0:T(8,128)S(1)}, f32[4,...) custom-call(f32[32,32,128]{2,1,0:T(8,128)S(1)} %get-tuple-element.63.refs_0_, ...), custom_call_target="tpu_custom_call" | custom-call | tf_op jit(solution)/shard_map/pallas_call | solution.py:24
  52.2 1.2 %collective-permute-start.19 = (f32[4,32,128]{2,1,0:T(8,128)S(1)}, f32[4,32,128]{2,1,0:T(8,128)S(1)}, u32[]{:S(2)}, u32[]{:S(2)}) collective-permute-start(f32[4,32,128]{2,1,0:T(8,128)S(1)} %get-tuple-element.79.refs_5_), channel_id=1, source_target_pairs={{0,2},{1,3},{2,0},{3,1},{4,6},{5,7},{6,4},{7,5},{8,10},{9,11},{10,... | collective-permute-start | bytes 196616 | tf_op jit(solution)/shard_map/ppermute | solution.py:77
  53.4 0.7 %collective-permute-start.18 = (f32[4,32,128]{2,1,0:T(8,128)S(1)}, f32[4,32,128]{2,1,0:T(8,128)S(1)}, u32[]{:S(2)}, u32[]{:S(2)}) collective-permute-start(f32[4,32,128]{2,1,0:T(8,128)S(1)} %get-tuple-element.79.refs_5_), channel_id=1, source_target_pairs={{0,1},{1,0},{2,3},{3,2},{4,5},{5,4},{6,7},{7,6},{8,9},{9,8},{10,11... | collective-permute-start | bytes 196616 | tf_op jit(solution)/shard_map/ppermute | solution.py:77
  54.0 2.5 %collective-permute-done.20.refs_11_ = f32[4,32,128]{2,1,0:T(8,128)S(1)} collective-permute-done((f32[4,32,128]{2,1,0:T(8,128)S(1)}, f32[4,32,128]{2,1,0:T(8,128)S(1)}, u32[]{:S(2)}, u32[]{:S(2)}) %collective-permute-start.20) | collective-permute-done | bytes 65568 | tf_op jit(solution)/shard_map/ppermute | solution.py:77
  56.5 0.9 %collective-permute-done.19.refs_10_ = f32[4,32,128]{2,1,0:T(8,128)S(1)} collective-permute-done((f32[4,32,128]{2,1,0:T(8,128)S(1)}, f32[4,32,128]{2,1,0:T(8,128)S(1)}, u32[]{:S(2)}, u32[]{:S(2)}) %collective-permute-start.19) | collective-permute-done | bytes 65568 | tf_op jit(solution)/shard_map/ppermute | solution.py:77
  57.5 1.2 %shard_map.109 = (f32[32,32,128]{2,1,0:T(8,128)}, f32[32,32,128]{2,1,0:T(8,128)}) custom-call(s32[1]{0:T(128)} %bitcast.group_ref, f32[32,32,128]{2,1,0:T(8,128)S(1)} %get-tuple-element.77.refs_0_, f32[32,32,128]{2,1,0:T(8,128)S(1)} %get-tuple-element.78.refs_1_, f32[32,32,128]{2,1,0:T(8,128)S(1)} %get-tuple-element.52.refs_2_, ...), custom_call_target="tpu_custom_call" | custom-call | tf_op jit(solution)/shard_map/pallas_call | solution.py:24
  (22 shorter events, 0.0 us)
Async XLA Ops:
  0.6 1.0 %copy-start = (f32[32,32,128]{2,1,0:T(8,128)S(1)}, f32[32,32,128]{2,1,0:T(8,128)}, u32[]{:S(2)}) copy-start(f32[32,32,128]{2,1,0:T(8,128)} %refs_0_.1) | copy-start | bytes 1572868
  1.7 1.0 %copy-start.2 = (f32[32,32,128]{2,1,0:T(8,128)S(1)}, f32[32,32,128]{2,1,0:T(8,128)}, u32[]{:S(2)}) copy-start(f32[32,32,128]{2,1,0:T(8,128)} %refs_1_.1) | copy-start | bytes 1572868
  2.7 1.0 %copy-start.4 = (f32[32,32,128]{2,1,0:T(8,128)S(1)}, f32[32,32,128]{2,1,0:T(8,128)}, u32[]{:S(2)}) copy-start(f32[32,32,128]{2,1,0:T(8,128)} %refs_3_.1) | copy-start | bytes 1572868
  3.8 12.6 %copy-start.3 = (f32[32,32,128]{2,1,0:T(8,128)S(1)}, f32[32,32,128]{2,1,0:T(8,128)}, u32[]{:S(2)}) copy-start(f32[32,32,128]{2,1,0:T(8,128)} %refs_1_.1) | copy-start | bytes 1572868
  3.8 12.6 %copy-start.5 = (f32[32,32,128]{2,1,0:T(8,128)S(1)}, f32[32,32,128]{2,1,0:T(8,128)}, u32[]{:S(2)}) copy-start(f32[32,32,128]{2,1,0:T(8,128)} %refs_3_.1) | copy-start | bytes 1572868
  3.8 12.6 %copy-start.6 = (f32[32,32,128]{2,1,0:T(8,128)S(1)}, f32[32,32,128]{2,1,0:T(8,128)}, u32[]{:S(2)}) copy-start(f32[32,32,128]{2,1,0:T(8,128)} %refs_2_.1) | copy-start | bytes 1572868
  4.1 12.3 %copy-start.1 = (f32[32,32,128]{2,1,0:T(8,128)S(1)}, f32[32,32,128]{2,1,0:T(8,128)}, u32[]{:S(2)}) copy-start(f32[32,32,128]{2,1,0:T(8,128)} %refs_0_.1) | copy-start | bytes 1572868
  4.1 12.2 %collective-permute-start = (f32[6,32,128]{2,1,0:T(8,128)S(1)}, f32[6,32,128]{2,1,0:T(8,128)S(1)}, u32[]{:S(2)}, u32[]{:S(2)}) collective-permute-start(f32[6,32,128]{2,1,0:T(8,128)S(1)} %get-tuple-element.45.refs_6_), channel_id=1, source_target_pairs={{0,16},{16,0},{1,17},{17,1},{2,18},{18,2},{3,19},{19,3},{4,20},{20... | collective-permute-start | bytes 294920 | tf_op jit(solution)/shard_map/ppermute | solution.py:60
  7.1 1.0 %copy-start.7 = (f32[32,32,128]{2,1,0:T(8,128)S(1)}, f32[32,32,128]{2,1,0:T(8,128)}, u32[]{:S(2)}) copy-start(f32[32,32,128]{2,1,0:T(8,128)} %c.1) | copy-start | bytes 1572868
  8.2 0.7 %copy-start.8 = (s32[32,128]{1,0:T(8,128)S(1)}, s32[32,128]{1,0:T(8,128)}, u32[]{:S(2)}) copy-start(s32[32,128]{1,0:T(8,128)} %surface.1) | copy-start | bytes 49156
  8.9 0.7 %copy-start.9 = (s32[32,128]{1,0:T(8,128)S(1)}, s32[32,128]{1,0:T(8,128)}, u32[]{:S(2)}) copy-start(s32[32,128]{1,0:T(8,128)} %lid.1) | copy-start | bytes 49156
  9.9 11.9 %collective-permute-start.5 = (f32[4,32,128]{2,1,0:T(8,128)S(1)}, f32[4,32,128]{2,1,0:T(8,128)S(1)}, u32[]{:S(2)}, u32[]{:S(2)}) collective-permute-start(f32[4,32,128]{2,1,0:T(8,128)S(1)} %get-tuple-element.54.refs_4_), channel_id=1, source_target_pairs={{0,3},{1,2},{2,1},{3,0},{4,7},{5,6},{6,5},{7,4},{8,11},{9,10},{10,... | collective-permute-start | bytes 196616 | tf_op jit(solution)/shard_map/ppermute | solution.py:77
  10.6 5.6 %collective-permute-start.1 = (f32[3,8,128]{2,1,0:T(8,128)S(1)}, f32[3,8,128]{2,1,0:T(8,128)S(1)}, u32[]{:S(2)}, u32[]{:S(2)}) collective-permute-start(f32[3,8,128]{2,1,0:T(8,128)S(1)} %get-tuple-element.46.refs_7_), channel_id=1, source_target_pairs={{0,4},{4,8},{8,12},{12,0},{1,5},{5,9},{9,13},{13,1},{2,6},{6,10},{... | collective-permute-start | bytes 36872 | tf_op jit(solution)/shard_map/ppermute | solution.py:62
  12.2 4.1 %collective-permute-start.2 = (f32[3,8,128]{2,1,0:T(8,128)S(1)}, f32[3,8,128]{2,1,0:T(8,128)S(1)}, u32[]{:S(2)}, u32[]{:S(2)}) collective-permute-start(f32[3,8,128]{2,1,0:T(8,128)S(1)} %get-tuple-element.47.refs_8_), channel_id=1, source_target_pairs={{4,0},{8,4},{12,8},{0,12},{5,1},{9,5},{13,9},{1,13},{6,2},{10,6},{... | collective-permute-start | bytes 36872 | tf_op jit(solution)/shard_map/ppermute | solution.py:62
  14.5 7.3 %collective-permute-start.4 = (f32[4,32,128]{2,1,0:T(8,128)S(1)}, f32[4,32,128]{2,1,0:T(8,128)S(1)}, u32[]{:S(2)}, u32[]{:S(2)}) collective-permute-start(f32[4,32,128]{2,1,0:T(8,128)S(1)} %get-tuple-element.54.refs_4_), channel_id=1, source_target_pairs={{0,2},{1,3},{2,0},{3,1},{4,6},{5,7},{6,4},{7,5},{8,10},{9,11},{10,... | collective-permute-start | bytes 196616 | tf_op jit(solution)/shard_map/ppermute | solution.py:77
  16.2 5.6 %collective-permute-start.3 = (f32[4,32,128]{2,1,0:T(8,128)S(1)}, f32[4,32,128]{2,1,0:T(8,128)S(1)}, u32[]{:S(2)}, u32[]{:S(2)}) collective-permute-start(f32[4,32,128]{2,1,0:T(8,128)S(1)} %get-tuple-element.54.refs_4_), channel_id=1, source_target_pairs={{0,1},{1,0},{2,3},{3,2},{4,5},{5,4},{6,7},{7,6},{8,9},{9,8},{10,11... | collective-permute-start | bytes 196616 | tf_op jit(solution)/shard_map/ppermute | solution.py:77
  19.7 3.9 %collective-permute-start.8 = (f32[4,32,128]{2,1,0:T(8,128)S(1)}, f32[4,32,128]{2,1,0:T(8,128)S(1)}, u32[]{:S(2)}, u32[]{:S(2)}) collective-permute-start(f32[4,32,128]{2,1,0:T(8,128)S(1)} %get-tuple-element.55.refs_5_), channel_id=1, source_target_pairs={{0,3},{1,2},{2,1},{3,0},{4,7},{5,6},{6,5},{7,4},{8,11},{9,10},{10,... | collective-permute-start | bytes 196616 | tf_op jit(solution)/shard_map/ppermute | solution.py:77
  20.6 5.0 %collective-permute-start.7 = (f32[4,32,128]{2,1,0:T(8,128)S(1)}, f32[4,32,128]{2,1,0:T(8,128)S(1)}, u32[]{:S(2)}, u32[]{:S(2)}) collective-permute-start(f32[4,32,128]{2,1,0:T(8,128)S(1)} %get-tuple-element.55.refs_5_), channel_id=1, source_target_pairs={{0,2},{1,3},{2,0},{3,1},{4,6},{5,7},{6,4},{7,5},{8,10},{9,11},{10,... | collective-permute-start | bytes 196616 | tf_op jit(solution)/shard_map/ppermute | solution.py:77
  21.8 3.8 %collective-permute-start.6 = (f32[4,32,128]{2,1,0:T(8,128)S(1)}, f32[4,32,128]{2,1,0:T(8,128)S(1)}, u32[]{:S(2)}, u32[]{:S(2)}) collective-permute-start(f32[4,32,128]{2,1,0:T(8,128)S(1)} %get-tuple-element.55.refs_5_), channel_id=1, source_target_pairs={{0,1},{1,0},{2,3},{3,2},{4,5},{5,4},{6,7},{7,6},{8,9},{9,8},{10,11... | collective-permute-start | bytes 196616 | tf_op jit(solution)/shard_map/ppermute | solution.py:77
  26.1 6.1 %collective-permute-start.9 = (f32[4,32,128]{2,1,0:T(8,128)S(1)}, f32[4,32,128]{2,1,0:T(8,128)S(1)}, u32[]{:S(2)}, u32[]{:S(2)}) collective-permute-start(f32[4,32,128]{2,1,0:T(8,128)S(1)} %get-tuple-element.58.refs_6_), channel_id=1, source_target_pairs={{0,16},{16,0},{1,17},{17,1},{2,18},{18,2},{3,19},{19,3},{4,20},{20... | collective-permute-start | bytes 196616 | tf_op jit(solution)/shard_map/ppermute | solution.py:60
  26.7 5.5 %collective-permute-start.10 = (f32[2,8,128]{2,1,0:T(8,128)S(1)}, f32[2,8,128]{2,1,0:T(8,128)S(1)}, u32[]{:S(2)}, u32[]{:S(2)}) collective-permute-start(f32[2,8,128]{2,1,0:T(8,128)S(1)} %get-tuple-element.59.refs_7_), channel_id=1, source_target_pairs={{0,4},{4,8},{8,12},{12,0},{1,5},{5,9},{9,13},{13,1},{2,6},{6,10},{... | collective-permute-start | bytes 24584 | tf_op jit(solution)/shard_map/ppermute | solution.py:62
  27.2 4.9 %collective-permute-start.11 = (f32[2,8,128]{2,1,0:T(8,128)S(1)}, f32[2,8,128]{2,1,0:T(8,128)S(1)}, u32[]{:S(2)}, u32[]{:S(2)}) collective-permute-start(f32[2,8,128]{2,1,0:T(8,128)S(1)} %get-tuple-element.60.refs_8_), channel_id=1, source_target_pairs={{4,0},{8,4},{12,8},{0,12},{5,1},{9,5},{13,9},{1,13},{6,2},{10,6},{... | collective-permute-start | bytes 24584 | tf_op jit(solution)/shard_map/ppermute | solution.py:62
  35.5 3.8 %collective-permute-start.14 = (f32[4,32,128]{2,1,0:T(8,128)S(1)}, f32[4,32,128]{2,1,0:T(8,128)S(1)}, u32[]{:S(2)}, u32[]{:S(2)}) collective-permute-start(f32[4,32,128]{2,1,0:T(8,128)S(1)} %get-tuple-element.67.refs_5_), channel_id=1, source_target_pairs={{0,3},{1,2},{2,1},{3,0},{4,7},{5,6},{6,5},{7,4},{8,11},{9,10},{10,... | collective-permute-start | bytes 196616 | tf_op jit(solution)/shard_map/ppermute | solution.py:77
  35.6 5.0 %collective-permute-start.13 = (f32[4,32,128]{2,1,0:T(8,128)S(1)}, f32[4,32,128]{2,1,0:T(8,128)S(1)}, u32[]{:S(2)}, u32[]{:S(2)}) collective-permute-start(f32[4,32,128]{2,1,0:T(8,128)S(1)} %get-tuple-element.67.refs_5_), channel_id=1, source_target_pairs={{0,2},{1,3},{2,0},{3,1},{4,6},{5,7},{6,4},{7,5},{8,10},{9,11},{10,... | collective-permute-start | bytes 196616 | tf_op jit(solution)/shard_map/ppermute | solution.py:77
  36.3 4.3 %collective-permute-start.12 = (f32[4,32,128]{2,1,0:T(8,128)S(1)}, f32[4,32,128]{2,1,0:T(8,128)S(1)}, u32[]{:S(2)}, u32[]{:S(2)}) collective-permute-start(f32[4,32,128]{2,1,0:T(8,128)S(1)} %get-tuple-element.67.refs_5_), channel_id=1, source_target_pairs={{0,1},{1,0},{2,3},{3,2},{4,5},{5,4},{6,7},{7,6},{8,9},{9,8},{10,11... | collective-permute-start | bytes 196616 | tf_op jit(solution)/shard_map/ppermute | solution.py:77
  41.1 7.0 %collective-permute-start.15 = (f32[4,32,128]{2,1,0:T(8,128)S(1)}, f32[4,32,128]{2,1,0:T(8,128)S(1)}, u32[]{:S(2)}, u32[]{:S(2)}) collective-permute-start(f32[4,32,128]{2,1,0:T(8,128)S(1)} %get-tuple-element.70.refs_6_), channel_id=1, source_target_pairs={{0,16},{16,0},{1,17},{17,1},{2,18},{18,2},{3,19},{19,3},{4,20},{20... | collective-permute-start | bytes 196616 | tf_op jit(solution)/shard_map/ppermute | solution.py:60
  42.6 5.4 %collective-permute-start.16 = (f32[2,8,128]{2,1,0:T(8,128)S(1)}, f32[2,8,128]{2,1,0:T(8,128)S(1)}, u32[]{:S(2)}, u32[]{:S(2)}) collective-permute-start(f32[2,8,128]{2,1,0:T(8,128)S(1)} %get-tuple-element.71.refs_7_), channel_id=1, source_target_pairs={{0,4},{4,8},{8,12},{12,0},{1,5},{5,9},{9,13},{13,1},{2,6},{6,10},{... | collective-permute-start | bytes 24584 | tf_op jit(solution)/shard_map/ppermute | solution.py:62
  43.1 5.0 %collective-permute-start.17 = (f32[2,8,128]{2,1,0:T(8,128)S(1)}, f32[2,8,128]{2,1,0:T(8,128)S(1)}, u32[]{:S(2)}, u32[]{:S(2)}) collective-permute-start(f32[2,8,128]{2,1,0:T(8,128)S(1)} %get-tuple-element.72.refs_8_), channel_id=1, source_target_pairs={{4,0},{8,4},{12,8},{0,12},{5,1},{9,5},{13,9},{1,13},{6,2},{10,6},{... | collective-permute-start | bytes 24584 | tf_op jit(solution)/shard_map/ppermute | solution.py:62
  52.2 4.4 %collective-permute-start.20 = (f32[4,32,128]{2,1,0:T(8,128)S(1)}, f32[4,32,128]{2,1,0:T(8,128)S(1)}, u32[]{:S(2)}, u32[]{:S(2)}) collective-permute-start(f32[4,32,128]{2,1,0:T(8,128)S(1)} %get-tuple-element.79.refs_5_), channel_id=1, source_target_pairs={{0,3},{1,2},{2,1},{3,0},{4,7},{5,6},{6,5},{7,4},{8,11},{9,10},{10,... | collective-permute-start | bytes 196616 | tf_op jit(solution)/shard_map/ppermute | solution.py:77
  52.2 5.3 %collective-permute-start.19 = (f32[4,32,128]{2,1,0:T(8,128)S(1)}, f32[4,32,128]{2,1,0:T(8,128)S(1)}, u32[]{:S(2)}, u32[]{:S(2)}) collective-permute-start(f32[4,32,128]{2,1,0:T(8,128)S(1)} %get-tuple-element.79.refs_5_), channel_id=1, source_target_pairs={{0,2},{1,3},{2,0},{3,1},{4,6},{5,7},{6,4},{7,5},{8,10},{9,11},{10,... | collective-permute-start | bytes 196616 | tf_op jit(solution)/shard_map/ppermute | solution.py:77
  53.4 4.1 %collective-permute-start.18 = (f32[4,32,128]{2,1,0:T(8,128)S(1)}, f32[4,32,128]{2,1,0:T(8,128)S(1)}, u32[]{:S(2)}, u32[]{:S(2)}) collective-permute-start(f32[4,32,128]{2,1,0:T(8,128)S(1)} %get-tuple-element.79.refs_5_), channel_id=1, source_target_pairs={{0,1},{1,0},{2,3},{3,2},{4,5},{5,4},{6,7},{7,6},{8,9},{9,8},{10,11... | collective-permute-start | bytes 196616 | tf_op jit(solution)/shard_map/ppermute | solution.py:77
where the time goes:
time: 59.1 us; the launch traced here: 58.7 us
  starting transfers between devices  24.3 us (41%)
  waiting for transfers between devices  14.5 us (25%)
  Pallas kernels  13.5 us (23%)
  local copies, waits for them, and re-layouts  5.61 us (9%)
  between operations  0.76 us (1%)
    pallas_call x8, Pallas kernels, call(): pl.pallas_call(kernel, out_shape=[jax.ShapeDtypeStruct(s, F32) for s in o...  13.5 us
    ppermute x12, waiting for transfers between devices, gather_lev(): got.append(lax.ppermute(message, 'lev', pairs))  10.4 us
    ppermute x3, starting transfers between devices, exchange(): lax.ppermute(messages[1], axis, down)  8.92 us
    ppermute x12, starting transfers between devices, gather_lev(): got.append(lax.ppermute(message, 'lev', pairs))  7.64 us
    unnamed x20, local copies, waits for them, and re-layouts  5.61 us
    ppermute x3, starting transfers between devices, exchange(): return [lax.ppermute(messages[0], axis, up)]  5.19 us
    ppermute x3, waiting for transfers between devices, exchange(): lax.ppermute(messages[0], axis, up)  4.11 us
    ppermute x3, starting transfers between devices, exchange(): lax.ppermute(messages[0], axis, up)  2.56 us
  transfers between devices with their start and end apart: 21, of which 9 were waited for; matrix products, arithmetic and copies ran while one was open for 0% of the time, Pallas kernels for 6%

commit v1 on v0

v1 whole, which is shorter than its diff:
```python
import functools

import jax
import jax.numpy as jnp
from jax import lax
from jax.experimental import pallas as pl
from jax.experimental.pallas import tpu as pltpu
from jax.sharding import PartitionSpec as P

SUBSTEPS = 3
H_STEP = 0.25
D_STEP = 0.25
V_STEP = 0.5
P_STEP = 0.5
F32 = jnp.float32
PAD = 8

VMEM = pl.BlockSpec(memory_space=pltpu.VMEM)
SMEM = pl.BlockSpec(memory_space=pltpu.SMEM)
HBM = pl.BlockSpec(memory_space=pltpu.HBM)


def call(kernel, outs, args, scratch=(), spaces=None, out_spaces=None):
    return list(
        pl.pallas_call(
            kernel,
            out_shape=[jax.ShapeDtypeStruct(s, F32) for s in outs],
            in_specs=spaces or [SMEM] + [VMEM] * (len(args) - 1),
            out_specs=out_spaces or [VMEM] * len(outs),
            scratch_shapes=list(scratch),
            compiler_params=pltpu.CompilerParams(vmem_limit_bytes=20 * 1024 * 1024),
        )(*args)
    )


class Halo:
    def __init__(self, axis, plane):
        self.axis, self.plane = axis, plane
        self.n = lax.axis_size(axis)
        self.count = 1 if self.n <= 2 else 2
        self.swap = self.n > 2 and self.n % 2 == 0

    def shapes(self, rows):
        return [(2 * rows,) + self.plane] if self.count == 1 else [(rows,) + self.plane] * 2

    def scratch(self, rows):
        return pltpu.VMEM((2, rows) + self.plane, F32)

    def write(self, refs, both, even):
        rows = both.shape[1]
        if self.count == 1:
            refs[0][:rows] = both[0]
            refs[0][rows:] = both[1]
        elif self.swap:
            refs[0][...] = jnp.where(even, both[0], both[1])
            refs[1][...] = jnp.where(even, both[1], both[0])
        else:
            refs[0][...] = both[0]
            refs[1][...] = both[1]

    def up(self, refs, r, even):
        if self.swap:
            return jnp.where(even, refs[0][r], refs[1][r])
        return refs[0][r]

    def down(self, refs, r, even):
        if self.swap:
            return jnp.where(even, refs[1][r], refs[0][r])
        return refs[0][refs[0].shape[0] // 2 + r] if self.count == 1 else refs[1][r]

    def low(self, refs, r, even):
        if self.swap:
            return jnp.where(even, refs[1][r], refs[0][r])
        return refs[0][r]

    def high(self, refs, r, even):
        if self.swap:
            return jnp.where(even, refs[0][r], refs[1][r])
        return refs[0][refs[0].shape[0] // 2 + r] if self.count == 1 else refs[1][r]

    def exchange(self, messages):
        n = self.n
        if n == 1:
            return messages
        if self.swap:
            first = [(i, i ^ 1) for i in range(n)]
            second = [(i, (i + 1) % n if i % 2 else (i - 1) % n) for i in range(n)]
            got = lax.ppermute(messages[1], self.axis, second)
            return [lax.ppermute(messages[0], self.axis, first), got]
        up = [(i, (i + 1) % n) for i in range(n)]
        if n == 2:
            return [lax.ppermute(messages[0], self.axis, up)]
        down = [(j, i) for i, j in up]
        return [lax.ppermute(messages[0], self.axis, up), lax.ppermute(messages[1], self.axis, down)]


def to_lev(message, m):
    n = lax.axis_size("lev")
    if n & (n - 1) == 0:
        return lax.ppermute(message, "lev", [(i, i ^ m) for i in range(n)])
    return lax.ppermute(message, "lev", [(i, (i + m) % n) for i in range(n)])


def source_of(group, m, n):
    return group ^ m if n & (n - 1) == 0 else (group - m) % n


def pack_columns(ref, picks, outs):
    depth, ni, nj = ref.shape
    per = nj // ni
    for b in range(depth // per):
        turned = ref[b * per : (b + 1) * per].reshape(per * ni, nj).T
        for c, out in zip(picks, outs):
            out[b : b + 1, :] = turned[c : c + 1, :]


def pack_pressure(press, both_x, both_y):
    ni, nj = press.shape[1:]
    for r in range(2):
        both_x[0, r] = press[:, ni - 2 + r, :]
        both_x[1, r] = press[:, r, :]
    pack_columns(press, (nj - 2, nj - 1, 0, 1), (both_y.at[0, 0], both_y.at[0, 1], both_y.at[1, 0], both_y.at[1, 1]))


def first_kernel(hx, hy, groups, where, *refs):
    zonal, merid, press, coupling, surface, lid = refs[:6]
    u, v, p = refs[6:9]
    mx, my = refs[9 : 9 + hx.count], refs[9 + hx.count : 9 + hx.count + hy.count]
    inv, mul, g0, gl, planes = refs[9 + hx.count + hy.count : 14 + hx.count + hy.count]
    both_x, both_y, c, ground, shut, sems = refs[14 + hx.count + hy.count :]
    pairs = [(press, p), (merid, v), (zonal, u), (coupling, c), (surface, ground), (lid, shut)]
    copies = [pltpu.make_async_copy(a, b, sems.at[n]) for n, (a, b) in enumerate(pairs)]
    for copy in copies:
        copy.start()
    ni, nj = p.shape[1:]
    copies[0].wait()
    pack_pressure(p, both_x, both_y)
    copies[1].wait()
    pack_columns(v, (nj - 1, 0), (both_y.at[0, 2], both_y.at[1, 2]))
    copies[2].wait()
    both_x[0, 2] = u[:, ni - 1, :]
    both_x[1, 2] = u[:, 0, :]
    hx.write(mx, both_x, where[1] == 0)
    hy.write(my, both_y, where[2] == 0)
    for copy in copies[3:]:
        copy.wait()
    factor(groups, where[0], c, ground, shut, inv, mul, g0, gl, planes)


def factor(groups, group, c, surface, lid, inv, mul, g0, gl, planes):
    depth, ni, nj = c.shape
    last, half = depth - 1, depth // 2
    bottom = group == 0
    top = group == groups - 1
    ground = surface[...] - group * depth
    lidf = jnp.where(top, lid[...].astype(F32), 0.0)

    def coupling(k):
        return jnp.where(ground <= k - 1, c[k], 0.0)

    def diag(k):
        low = c[k] if k > 0 else jnp.where(bottom, c[k], 0.0)
        high = c[k + 1] if k < last else lidf * c[k]
        return 1.0 + low + high

    lo, hi = None, None
    for s in range(half):
        k, j = s, last - s
        d_lo, d_hi = diag(k), diag(j)
        if s:
            e_lo = coupling(k)
            m_lo = e_lo * lo
            mul[k] = m_lo
            d_lo = d_lo - e_lo * m_lo
            e_hi = coupling(j + 1)
            m_hi = e_hi * hi
            mul[j + 1] = m_hi
            d_hi = d_hi - e_hi * m_hi
        if j == half:
            e_mid = coupling(half)
            lo = jnp.where(ground <= k, 1.0 / d_lo, 0.0)
            m_mid = e_mid * lo
            mul[half] = m_mid
            d_hi = d_hi - e_mid * m_mid
        else:
            lo = jnp.where(ground <= k, 1.0 / d_lo, 0.0)
        hi = jnp.where(ground <= j, 1.0 / d_hi, 0.0)
        inv[k] = lo
        inv[j] = hi
    one = jnp.ones((ni, nj), F32)
    t0 = [one] + [None] * (half - 1)
    tl = [one] + [None] * (half - 1)
    for s in range(1, half):
        t0[s] = mul[s] * t0[s - 1]
        tl[s] = mul[last - s + 1] * tl[s - 1]
        g0[s] = t0[s]
        gl[last - s] = tl[s]
    g0[0] = one
    gl[last] = one
    xh0 = inv[half] * (mul[half] * t0[half - 1])
    xhl = inv[half] * tl[half - 1]
    xk0 = inv[half - 1] * t0[half - 1] + mul[half] * xh0
    xkl = mul[half] * xhl
    g0[half], gl[half] = xh0, xhl
    g0[half - 1], gl[half - 1] = xk0, xkl
    for s in range(1, half):
        k, j = half - 1 - s, half + s
        xk0 = inv[k] * g0[k] + mul[k + 1] * xk0
        xkl = mul[k + 1] * xkl
        xh0 = mul[j] * xh0
        xhl = inv[j] * gl[j] + mul[j] * xhl
        g0[k], gl[k] = xk0, xkl
        g0[j], gl[j] = xh0, xhl
    planes[0] = g0[0]
    planes[1] = g0[last]
    planes[2] = gl[last]
    planes[3] = c[0]


def condense(group, st, cf):
    half = group // 2
    near = jnp.where(half == 0, 2, 0)
    inner = 1 + half
    outer = 3 * half

    def half_of(inner, outer, near):
        odd = jnp.where(inner == 1, 1, 3)
        c = st[odd, 3]
        x = st[inner, 1]
        kappa = c / (1.0 + c * (st[outer, near] + st[inner, 2 - near]))
        return kappa, st[inner, near] - kappa * x * x, x

    kappa, mine, x = half_of(inner, outer, near)
    _, other, _ = half_of(3 - inner, 3 - outer, 2 - near)
    c = st[2, 3]
    cf[0] = kappa
    cf[1] = mine
    cf[2] = other
    cf[3] = c / (1.0 + c * (mine + other))
    cf[4] = x
    cf[5] = st[outer, near]
    cf[6] = st[inner, 2 - near]


def spread_setup(groups, group, own, got, st):
    st[group] = own[...]
    for m in range(1, groups):
        st[source_of(group, m, groups)] = got[m - 1][...]


def advance_kernel(first, hx, hy, groups, where, *refs):
    refs = list(refs)
    take = lambda n: [refs.pop(0) for _ in range(n)]
    zonal, merid, vert, press, inv, mul = take(6)
    ox, oy = take(hx.count), take(hy.count)
    rx, ry = take(hx.count), take(hy.count)
    paired = groups == 4
    if first:
        own_s = take(1)[0]
        got_s = take(groups - 1)
    else:
        uh, vh = take(2)
        cf = take(1)[0] if paired else None
    zonal_out, merid_out, y_out, part, planes, uh_out, vh_out = take(7)
    across = take(1)[0] if paired else None
    if first:
        st = take(1)[0]
        cf = take(1)[0] if paired else None
    pe, ue, tsq = take(3)
    depth, ni, nj = press.shape
    last, half, per = depth - 1, depth // 2, nj // ni
    group, even_x, even_y = where[0], where[1] == 0, where[2] == 0
    if first:
        spread_setup(groups, group, own_s, got_s, st)
        if paired:
            condense(group, st, cf)

    u_lo = hx.low(rx, 2, even_x) if first else uh[0]
    u_hi = hx.high(rx, 2, even_x) if first else uh[1]
    u_lo = u_lo - H_STEP * (hx.down(ox, 0, even_x) - hx.low(rx, 0, even_x))
    u_hi = u_hi - H_STEP * (hx.high(rx, 1, even_x) - hx.up(ox, 1, even_x))
    uh_out[0], uh_out[1] = u_lo, u_hi
    v_lo = hy.low(ry, 2, even_y) if first else vh[0]
    v_hi = hy.high(ry, 2, even_y) if first else vh[1]
    v_lo = v_lo - H_STEP * (hy.down(oy, 0, even_y) - hy.low(ry, 0, even_y))
    v_hi = v_hi - H_STEP * (hy.high(ry, 1, even_y) - hy.up(oy, 1, even_y))
    vh_out[0], vh_out[1] = v_lo, v_hi

    ue[:, PAD - 1, :] = u_lo
    ue[:, PAD + ni, :] = u_hi
    pe[:, PAD - 1, :] = hx.low(rx, 1, even_x)
    pe[:, PAD + ni, :] = hx.high(rx, 0, even_x)
    p_lo, p_hi = hy.low(ry, 1, even_y), hy.high(ry, 0, even_y)
    rows = per * ni
    src = lax.broadcasted_iota(jnp.int32, (2 * nj, nj), 0) % nj
    dst = lax.broadcasted_iota(jnp.int32, (2 * nj, nj), 1)
    diff = jnp.where(src == dst + 1, 1.0, jnp.where(src == dst - 1, -1.0, 0.0)).astype(jnp.bfloat16)

    def lane_difference(x):
        high = x.astype(jnp.bfloat16)
        low = (x - high.astype(F32)).astype(jnp.bfloat16)
        return jnp.dot(jnp.concatenate([high, low], 1), diff, preferred_element_type=F32)

    tsq[...] = jnp.zeros(tsq.shape, F32)
    for b in range(depth // per):
        here = slice(b * per, (b + 1) * per)
        tsq[0, 0:1, :] = -p_lo[b : b + 1]
        tsq[0, nj - 1 : nj, :] = p_hi[b : b + 1]
        tsq[1, 0:1, :] = -v_lo[b : b + 1]
        tsq[1, nj - 1 : nj, :] = v_hi[b : b + 1]
        p = press[here]
        pe[here, PAD : PAD + ni, :] = p
        p = p.reshape(rows, nj)
        u = zonal[here] - H_STEP * (pe[here, PAD + 1 : PAD + 1 + ni, :] - pe[here, PAD - 1 : PAD - 1 + ni, :])
        zonal_out[here] = u
        ue[here, PAD : PAD + ni, :] = u
        v = merid[here].reshape(rows, nj) - H_STEP * (lane_difference(p) + tsq[0].T)
        merid_out[here] = v.reshape(per, ni, nj)
        spread = (ue[here, PAD + 1 : PAD + 1 + ni, :] - ue[here, PAD - 1 : PAD - 1 + ni, :]).reshape(rows, nj)
        spread = spread + (lane_difference(v) + tsq[1].T)
        part[here] = (p - D_STEP * spread).reshape(per, ni, nj)

    lo = vert[0] - V_STEP * part[1]
    hi = vert[last] + V_STEP * part[last - 1]
    y_out[0], y_out[last] = lo, hi
    for s in range(1, half):
        k, j = s, last - s
        lo = (vert[k] - V_STEP * (part[k + 1] - part[k - 1])) + mul[k] * lo
        hi = (vert[j] - V_STEP * (part[j + 1] - part[j - 1])) + mul[j + 1] * hi
        y_out[k], y_out[j] = lo, hi
    hi = inv[half] * (hi + mul[half] * lo)
    lo = inv[half - 1] * lo + mul[half] * hi
    y_out[half], y_out[half - 1] = hi, lo
    for s in range(1, half):
        k, j = half - 1 - s, half + s
        lo = inv[k] * y_out[k] + mul[k + 1] * lo
        hi = inv[j] * y_out[j] + mul[j] * hi
        y_out[k], y_out[j] = lo, hi
    p_first, p_last = part[0], part[last]
    planes[0], planes[1] = lo, hi
    planes[2], planes[3] = p_first, p_last
    if paired:
        lower = group < 2
        sign = jnp.where(lower, V_STEP, -V_STEP)
        y_near, y_far = jnp.where(lower, hi, lo), jnp.where(lower, lo, hi)
        p_near, p_far = jnp.where(lower, p_last, p_first), jnp.where(lower, p_first, p_last)
        gain = cf[4] * cf[0]
        inside = y_near - gain * (cf[5] * (sign * p_far) + y_far)
        outside = cf[4] * (sign * p_near) + gain * (y_near - cf[6] * (sign * p_near))
        across[0] = jnp.where((group == 1) | (group == 2), inside, outside)
        across[1] = p_near


def paired_sources(group, cf, own, mate, crossed, lv):
    lower = group < 2
    is_inner = (group == 1) | (group == 2)
    sign = jnp.where(lower, V_STEP, -V_STEP)
    near = jnp.where(lower, 1, 0)
    slot = jnp.where(is_inner, 0, 1)
    lv[slot] = own[...]
    lv[1 - slot] = mate[...]
    kappa, mine, other, gain, x, g_out, g_in = (cf[n] for n in range(7))
    y_in_near, y_in_far, y_out = lv[0, near], lv[0, 1 - near], lv[1, near]
    p_in_near = sign * lv[0, 2 + near]
    p_in_far = sign * lv[0, 3 - near]
    p_out = sign * lv[1, 2 + near]
    flux = kappa * ((y_out - g_out * p_in_far) - (y_in_far + g_in * p_out))
    here = y_in_near + x * (p_out + flux)
    there = crossed[0][0] + crossed[1][0]
    p_there = sign * jnp.where(is_inner, crossed[1][1], crossed[0][1])
    middle = gain * ((there - here) + (other * p_in_near + mine * p_there))
    n_here = middle - p_there
    n_there = p_in_near - middle
    flux = flux - kappa * x * n_here
    in_far = p_out + flux
    out_near = -(p_in_far + flux)
    near_source = jnp.where(is_inner, n_here, out_near)
    far_source = jnp.where(is_inner, in_far, 0.0)
    alpha = jnp.where(lower, far_source, near_source)
    beta = jnp.where(lower, near_source, far_source)
    under = jnp.where(
        group == 1,
        y_out + g_out * out_near,
        jnp.where(
            group == 2,
            there + other * n_there,
            jnp.where(group == 3, y_in_far + g_in * in_far + x * n_here, 0.0),
        ),
    )
    return alpha, beta, under


def chain_sources(groups, group, st, own, got, lv):
    lv[group] = own[...]
    for m in range(1, groups):
        lv[source_of(group, m, groups)] = got[m - 1][...]
    zero = jnp.zeros(own.shape[1:], F32)
    z_top, z_bot = [], []
    for g in range(groups):
        below = V_STEP * lv[g - 1, 3] if g else zero
        above = V_STEP * lv[g + 1, 2] if g < groups - 1 else zero
        z_top.append(lv[g, 0] + st[g, 0] * below - st[g, 1] * above)
        z_bot.append(lv[g, 1] + st[g, 1] * below - st[g, 2] * above)
    ratios, parts = [zero], [zero]
    for g in range(1, groups):
        cg = st[g, 3]
        down = cg * st[g - 1, 1]
        pivot = 1.0 / (1.0 + cg * (st[g - 1, 2] + st[g, 0]) - down * ratios[-1])
        parts.append((cg * (z_bot[g - 1] - z_top[g]) + down * parts[-1]) * pivot)
        ratios.append(cg * st[g, 1] * pivot)
    flux = [zero] * (groups + 1)
    for g in range(groups - 1, 0, -1):
        flux[g] = parts[g] + ratios[g] * flux[g + 1]
    alpha, beta, under = zero, zero, zero
    for g in range(groups):
        mine = group == g
        if g:
            alpha = jnp.where(mine, V_STEP * lv[g - 1, 3] + flux[g], alpha)
            bot = z_bot[g - 1] + st[g - 1, 1] * flux[g - 1] - st[g - 1, 2] * flux[g]
            under = jnp.where(mine, bot, under)
        if g < groups - 1:
            beta = jnp.where(mine, -(V_STEP * lv[g + 1, 2] + flux[g + 1]), beta)
    return alpha, beta, under


def finish_kernel(groups, final, hx, hy, where, *refs):
    refs = list(refs)
    take = lambda n: [refs.pop(0) for _ in range(n)]
    y, part, g0, gl, system, own = take(6)
    got = take(groups - 1)
    vert_out, press_out = take(2)
    mx, my = ([], []) if final else (take(hx.count), take(hy.count))
    lv = take(1)[0]
    depth, ni, nj = y.shape
    group = where[0]
    if groups == 4:
        alpha, beta, under = paired_sources(group, system, own, got[0], got[1:], lv)
    else:
        alpha, beta, under = chain_sources(groups, group, system, own, got, lv)

    def level(k, w_prev):
        w = y[k] + g0[k] * alpha + gl[k] * beta
        vert_out[k] = w
        press_out[k] = part[k] - P_STEP * (w - w_prev)
        return w

    lax.fori_loop(0, depth, level, under, unroll=4)
    if final:
        return
    both_x, both_y = take(2)
    pack_pressure(press_out, both_x, both_y)
    hx.write(mx, both_x, where[1] == 0)
    hy.write(my, both_y, where[2] == 0)


def body(zonal, meridional, vertical, pressure, coupling, surface, lid_flag):
    depth, ni, nj = coupling.shape
    full, four, two = (depth, ni, nj), (4, ni, nj), (2, ni, nj)
    groups = lax.axis_size("lev")
    paired = groups == 4
    hx = Halo("gx", (depth, nj))
    hy = Halo("gy", (depth // (nj // ni), nj))
    where = jnp.stack([lax.axis_index("lev"), lax.axis_index("gx") % 2, lax.axis_index("gy") % 2]).astype(jnp.int32)

    results = call(
        functools.partial(first_kernel, hx, hy, groups),
        [full] * 3 + hx.shapes(3) + hy.shapes(3) + [full] * 4 + [four],
        [where, zonal, meridional, pressure, coupling, surface, lid_flag],
        scratch=[
            hx.scratch(3),
            hy.scratch(3),
            pltpu.VMEM(full, F32),
            pltpu.VMEM(surface.shape, surface.dtype),
            pltpu.VMEM(lid_flag.shape, lid_flag.dtype),
            pltpu.SemaphoreType.DMA((6,)),
        ],
        spaces=[SMEM] + [HBM] * 6,
    )
    zonal, meridional, pressure = results[:3]
    ox, oy = results[3 : 3 + hx.count], results[3 + hx.count : 3 + hx.count + hy.count]
    inv, mul, g0, gl, own_s = results[3 + hx.count + hy.count :]
    ry, rx = hy.exchange(oy), hx.exchange(ox)
    got_s = [to_lev(own_s, m) for m in range(1, groups)]
    system = uh = vh = None
    for substep in range(SUBSTEPS):
        first, final = substep == 0, substep == SUBSTEPS - 1
        args = [where, zonal, meridional, vertical, pressure, inv, mul] + ox + oy + rx + ry
        outs = [full] * 4 + [four, (2,) + hx.plane, (2,) + hy.plane]
        if first:
            args += [own_s] + got_s
        else:
            args += [uh, vh] + ([system] if paired else [])
        if paired:
            outs += [two]
        if first:
            outs += [(groups, 4, ni, nj)] + ([(7, ni, nj)] if paired else [])
        results = call(
            functools.partial(advance_kernel, first, hx, hy, groups),
            outs,
            args,
            scratch=[
                pltpu.VMEM((depth, ni + 2 * PAD, nj), F32),
                pltpu.VMEM((depth, ni + 2 * PAD, nj), F32),
                pltpu.VMEM((2, nj, nj), F32),
            ],
        )
        zonal, meridional, y, part, own, uh, vh = results[:7]
        if first:
            system = results[-1]
        if paired:
            across = results[7]
            got = [to_lev(own, 1), to_lev(across, 2), to_lev(across, 3)]
        else:
            got = [to_lev(own, m) for m in range(1, groups)]
        outs, scratch = [full, full], [pltpu.VMEM((groups, 4, ni, nj), F32)]
        if not final:
            outs += hx.shapes(2) + hy.shapes(2)
            scratch += [hx.scratch(2), hy.scratch(2)]
        results = call(
            functools.partial(finish_kernel, groups, final, hx, hy),
            outs,
            [where, y, part, g0, gl, system, own] + got,
            scratch=scratch,
        )
        vertical, pressure = results[:2]
        if not final:
            ox, oy = results[2 : 2 + hx.count], results[2 + hx.count :]
            ry, rx = hy.exchange(oy), hx.exchange(ox)
    return (zonal, meridional, vertical, pressure)


def solution(mesh):
    block = P("lev", "gx", "gy")
    plane = P("gx", "gy")
    return jax.shard_map(
        body,
        mesh=mesh,
        in_specs=(block,) * 5 + (plane,) * 2,
        out_specs=(block,) * 4,
        check_vma=False,
    )
```

time: 59.1 us -> 60.8 us (1.029)
  waiting for transfers between devices: 14.5 us -> 17.5 us
  Pallas kernels: 13.5 us -> 11 us
  starting transfers between devices: 24.3 us -> 26.2 us
  local copies, waits for them, and re-layouts: 5.61 us -> 4.8 us
    ppermute x21, waiting for transfers between devices: 14.5 us -> 17.5 us  [the longest x12 9.16 us: to_lev(): return lax.ppermute(message, 'lev', [(i, i ^ m) for i in range(n)])]
    pallas_call x8 -> x7, Pallas kernels: 13.5 us -> 11 us  [call(): pl.pallas_call(kernel, out_shape=[jax.ShapeDtypeStruct(s, F32) for s in o...]
    ppermute x21, starting transfers between devices: 24.3 us -> 26.2 us  [the longest x3 10.1 us: exchange(): got = lax.ppermute(messages[1], self.axis, second)]
    unnamed x20 -> x14, local copies, waits for them, and re-layouts: 5.61 us -> 4.8 us
  transfers between devices with their start and end apart: 21 -> 21, of which waited for: 9 -> 10; matrix products, arithmetic and copies ran while one was open for 0% -> 0% of each run, Pallas kernels for 6% -> 0%
where the time goes in v1:
time: 60.8 us; the launch traced here: 60.4 us
  starting transfers between devices  26.2 us (43%)
  waiting for transfers between devices  17.5 us (29%)
  Pallas kernels  11 us (18%)
  local copies, waits for them, and re-layouts  4.8 us (8%)
  between operations  0.75 us (1%)
    pallas_call x7, Pallas kernels, call(): pl.pallas_call(kernel, out_shape=[jax.ShapeDtypeStruct(s, F32) for s in o...  11 us
    ppermute x3, starting transfers between devices, exchange(): got = lax.ppermute(messages[1], self.axis, second)  10.1 us
    ppermute x12, waiting for transfers between devices, to_lev(): return lax.ppermute(message, 'lev', [(i, i ^ m) for i in range(n)])  9.16 us
    ppermute x12, starting transfers between devices, to_lev(): return lax.ppermute(message, 'lev', [(i, i ^ m) for i in range(n)])  8.34 us
    ppermute x3, waiting for transfers between devices, exchange(): got = lax.ppermute(messages[1], self.axis, second)  6.22 us
    ppermute x3, starting transfers between devices, exchange(): return [lax.ppermute(messages[0], self.axis, up)]  5.25 us
    unnamed x14, local copies, waits for them, and re-layouts  4.8 us
    ppermute x3, starting transfers between devices, exchange(): return [lax.ppermute(messages[0], self.axis, first), got]  2.48 us
  transfers between devices with their start and end apart: 21, of which 10 were waited for; matrix products, arithmetic and copies ran while one was open for 0% of the time, Pallas kernels for 0%

profile of v1, /device:TPU:0, one launch (start us, length us, event | category | flops | bytes accessed | tf_op | source)
XLA Modules:
  0.0 60.4 jit_solution(12298488862508979380)
XLA Ops:
  0.7 0.1 pad_add_fusion.where
  0.7 0.6 %copy-done.5 = s32[32,128]{1,0:T(8,128)S(1)} copy-done((s32[32,128]{1,0:T(8,128)S(1)}, s32[32,128]{1,0:T(8,128)}, u32[]{:S(2)}) %copy-start.5) | copy-done | bytes 16408
  1.4 0.0 copy-done.6
  1.4 1.0 %copy-done = f32[32,32,128]{2,1,0:T(8,128)S(1)} copy-done((f32[32,32,128]{2,1,0:T(8,128)S(1)}, f32[32,32,128]{2,1,0:T(8,128)}, u32[]{:S(2)}) %copy-start) | copy-done | bytes 524312
  2.4 1.0 %copy-done.1 = f32[32,32,128]{2,1,0:T(8,128)S(1)} copy-done((f32[32,32,128]{2,1,0:T(8,128)S(1)}, f32[32,32,128]{2,1,0:T(8,128)}, u32[]{:S(2)}) %copy-start.1) | copy-done | bytes 524312
  3.5 1.0 %copy-done.2 = f32[32,32,128]{2,1,0:T(8,128)S(1)} copy-done((f32[32,32,128]{2,1,0:T(8,128)S(1)}, f32[32,32,128]{2,1,0:T(8,128)}, u32[]{:S(2)}) %copy-start.2) | copy-done | bytes 524312
  4.5 1.0 %copy-done.3 = f32[32,32,128]{2,1,0:T(8,128)S(1)} copy-done((f32[32,32,128]{2,1,0:T(8,128)S(1)}, f32[32,32,128]{2,1,0:T(8,128)}, u32[]{:S(2)}) %copy-start.3) | copy-done | bytes 524312
  5.5 1.5 %shard_map.102 = (f32[32,32,128]{2,1,0:T(8,128)S(1)}, f32[32,32,128]{2,1,0:T(8,128)S(1)}, f32[32,32,128]{2,1,0:T(8,128)S(1)}, f32[6,32,128]{2,1,0:T(8,128)S(1)},...) custom-call(s32[3]{0:T(128)S(1)} %pad_add_fusion.where, ...), custom_call_target="tpu_custom_call" | custom-call | tf_op jit(solution)/shard_map/pallas_call | solution.py:25
  7.1 3.0 %collective-permute-start = (f32[6,32,128]{2,1,0:T(8,128)S(1)}, f32[6,32,128]{2,1,0:T(8,128)S(1)}, u32[]{:S(2)}, u32[]{:S(2)}) collective-permute-start(f32[6,32,128]{2,1,0:T(8,128)S(1)} %get-tuple-element.55.refs_6_), channel_id=1, source_target_pairs={{0,16},{16,0},{1,17},{17,1},{2,18},{18,2},{3,19},{19,3},{4,20},{20... | collective-permute-start | bytes 294920 | tf_op jit(solution)/shard_map/ppermute | solution.py:92
  10.1 0.7 %collective-permute-start.5 = (f32[4,32,128]{2,1,0:T(8,128)S(1)}, f32[4,32,128]{2,1,0:T(8,128)S(1)}, u32[]{:S(2)}, u32[]{:S(2)}) collective-permute-start(f32[4,32,128]{2,1,0:T(8,128)S(1)} %get-tuple-element.58.refs_12_), channel_id=1, source_target_pairs={{0,3},{1,2},{2,1},{3,0},{4,7},{5,6},{6,5},{7,4},{8,11},{9,10},{10,... | collective-permute-start | bytes 196616 | tf_op jit(solution)/shard_map/ppermute | solution.py:100
  10.8 0.8 %collective-permute-start.4 = (f32[4,32,128]{2,1,0:T(8,128)S(1)}, f32[4,32,128]{2,1,0:T(8,128)S(1)}, u32[]{:S(2)}, u32[]{:S(2)}) collective-permute-start(f32[4,32,128]{2,1,0:T(8,128)S(1)} %get-tuple-element.58.refs_12_), channel_id=1, source_target_pairs={{0,2},{1,3},{2,0},{3,1},{4,6},{5,7},{6,4},{7,5},{8,10},{9,11},{10,... | collective-permute-start | bytes 196616 | tf_op jit(solution)/shard_map/ppermute | solution.py:100
  11.6 0.3 collective-permute-start.3
  12.0 1.6 %collective-permute-start.1 = (f32[3,8,128]{2,1,0:T(8,128)S(1)}, f32[3,8,128]{2,1,0:T(8,128)S(1)}, u32[]{:S(2)}, u32[]{:S(2)}) collective-permute-start(f32[3,8,128]{2,1,0:T(8,128)S(1)} %get-tuple-element.56.refs_7_), channel_id=1, source_target_pairs={{0,4},{4,0},{8,12},{12,8},{1,5},{5,1},{9,13},{13,9},{2,6},{6,2},{1... | collective-permute-start | bytes 36872 | tf_op jit(solution)/shard_map/ppermute | solution.py:89
  13.5 2.1 %collective-permute-done.1.refs_10_ = f32[3,8,128]{2,1,0:T(8,128)S(1)} collective-permute-done((f32[3,8,128]{2,1,0:T(8,128)S(1)}, f32[3,8,128]{2,1,0:T(8,128)S(1)}, u32[]{:S(2)}, u32[]{:S(2)}) %collective-permute-start.1) | collective-permute-done | bytes 12320 | tf_op jit(solution)/shard_map/ppermute | solution.py:89
  15.7 3.6 %collective-permute-start.2 = (f32[3,8,128]{2,1,0:T(8,128)S(1)}, f32[3,8,128]{2,1,0:T(8,128)S(1)}, u32[]{:S(2)}, u32[]{:S(2)}) collective-permute-start(f32[3,8,128]{2,1,0:T(8,128)S(1)} %get-tuple-element.57.refs_8_), channel_id=1, source_target_pairs={{0,12},{4,8},{8,4},{12,0},{1,13},{5,9},{9,5},{13,1},{2,14},{6,10},... | collective-permute-start | bytes 36872 | tf_op jit(solution)/shard_map/ppermute | solution.py:88
  19.3 1.9 %collective-permute-done.2.refs_11_ = f32[3,8,128]{2,1,0:T(8,128)S(1)} collective-permute-done((f32[3,8,128]{2,1,0:T(8,128)S(1)}, f32[3,8,128]{2,1,0:T(8,128)S(1)}, u32[]{:S(2)}, u32[]{:S(2)}) %collective-permute-start.2) | collective-permute-done | bytes 12320 | tf_op jit(solution)/shard_map/ppermute | solution.py:88
  21.1 0.0 collective-permute-done.5.refs_15_
  21.2 2.2 %shard_map.103 = (f32[32,32,128]{2,1,0:T(8,128)S(1)}, f32[32,32,128]{2,1,0:T(8,128)S(1)}, f32[32,32,128]{2,1,0:T(8,128)S(1)}, f32[32,32,128]{2,1,0:T(8,128)S(1)}...) custom-call(s32[3]{0:T(128)S(1)} %pad_add_fusion.where, ...), custom_call_target="tpu_custom_call" | custom-call | tf_op jit(solution)/shard_map/pallas_call | solution.py:25
  23.4 1.6 %collective-permute-start.8 = (f32[2,32,128]{2,1,0:T(8,128)S(1)}, f32[2,32,128]{2,1,0:T(8,128)S(1)}, u32[]{:S(2)}, u32[]{:S(2)}) collective-permute-start(f32[2,32,128]{2,1,0:T(8,128)S(1)} %get-tuple-element.67), channel_id=1, source_target_pairs={{0,3},{1,2},{2,1},{3,0},{4,7},{5,6},{6,5},{7,4},{8,11},{9,10},{10,... | collective-permute-start | bytes 98312 | tf_op jit(solution)/shard_map/ppermute | solution.py:100
  25.0 0.5 collective-permute-start.7
  25.5 1.2 %collective-permute-done.8.refs_8_ = f32[2,32,128]{2,1,0:T(8,128)S(1)} collective-permute-done((f32[2,32,128]{2,1,0:T(8,128)S(1)}, f32[2,32,128]{2,1,0:T(8,128)S(1)}, u32[]{:S(2)}, u32[]{:S(2)}) %collective-permute-start.8) | collective-permute-done | bytes 32800 | tf_op jit(solution)/shard_map/ppermute | solution.py:100
  26.7 2.2 %collective-permute-done.7.refs_7_ = f32[2,32,128]{2,1,0:T(8,128)S(1)} collective-permute-done((f32[2,32,128]{2,1,0:T(8,128)S(1)}, f32[2,32,128]{2,1,0:T(8,128)S(1)}, u32[]{:S(2)}, u32[]{:S(2)}) %collective-permute-start.7) | collective-permute-done | bytes 32800 | tf_op jit(solution)/shard_map/ppermute | solution.py:100
  28.9 0.0 collective-permute-done.6.refs_6_
  28.9 1.0 %shard_map.104 = (f32[32,32,128]{2,1,0:T(8,128)S(1)}, f32[32,32,128]{2,1,0:T(8,128)S(1)}, f32[4,32,128]{2,1,0:T(8,128)S(1)}, f32[2,8,128]{2,1,0:T(8,128)S(1)}, f32[2,8,128]{2,1,0:T(8,128)S(1)}) custom-call(s32[3]{0:T(128)S(1)} %pad_add_fusion.where, f32[32,32,128]{2,1,0:T(8,128)S(1)} %get-tuple-element.61.refs_0_, ...), custom_call_target="tpu_custom_call" | custom-call | tf_op jit(solution)/shard_map/pallas_call | solution.py:25
  29.9 0.6 collective-permute-start.9
  30.5 0.0 collective-permute-start.10
  30.5 3.6 %collective-permute-start.11 = (f32[2,8,128]{2,1,0:T(8,128)S(1)}, f32[2,8,128]{2,1,0:T(8,128)S(1)}, u32[]{:S(2)}, u32[]{:S(2)}) collective-permute-start(f32[2,8,128]{2,1,0:T(8,128)S(1)} %get-tuple-element.72.refs_8_), channel_id=1, source_target_pairs={{0,12},{4,8},{8,4},{12,0},{1,13},{5,9},{9,5},{13,1},{2,14},{6,10},... | collective-permute-start | bytes 24584 | tf_op jit(solution)/shard_map/ppermute | solution.py:88
  34.1 0.0 collective-permute-done.10.refs_10_
  34.1 1.8 %collective-permute-done.11.refs_11_ = f32[2,8,128]{2,1,0:T(8,128)S(1)} collective-permute-done((f32[2,8,128]{2,1,0:T(8,128)S(1)}, f32[2,8,128]{2,1,0:T(8,128)S(1)}, u32[]{:S(2)}, u32[]{:S(2)}) %collective-permute-start.11) | collective-permute-done | bytes 8224 | tf_op jit(solution)/shard_map/ppermute | solution.py:88
  35.9 1.5 %shard_map.105 = (f32[32,32,128]{2,1,0:T(8,128)S(1)}, f32[32,32,128]{2,1,0:T(8,128)S(1)}, f32[32,32,128]{2,1,0:T(8,128)S(1)}, f32[32,32,128]{2,1,0:T(8,128)S(1)}...) custom-call(s32[3]{0:T(128)S(1)} %pad_add_fusion.where, ...), custom_call_target="tpu_custom_call" | custom-call | tf_op jit(solution)/shard_map/pallas_call | solution.py:25
  37.5 0.1 collective-permute-start.12
  37.5 0.5 collective-permute-start.14
  38.0 1.7 %collective-permute-start.13 = (f32[2,32,128]{2,1,0:T(8,128)S(1)}, f32[2,32,128]{2,1,0:T(8,128)S(1)}, u32[]{:S(2)}, u32[]{:S(2)}) collective-permute-start(f32[2,32,128]{2,1,0:T(8,128)S(1)} %get-tuple-element.80), channel_id=1, source_target_pairs={{0,2},{1,3},{2,0},{3,1},{4,6},{5,7},{6,4},{7,5},{8,10},{9,11},{10,... | collective-permute-start | bytes 98312 | tf_op jit(solution)/shard_map/ppermute | solution.py:100
  39.7 1.3 %collective-permute-done.14.refs_8_ = f32[2,32,128]{2,1,0:T(8,128)S(1)} collective-permute-done((f32[2,32,128]{2,1,0:T(8,128)S(1)}, f32[2,32,128]{2,1,0:T(8,128)S(1)}, u32[]{:S(2)}, u32[]{:S(2)}) %collective-permute-start.14) | collective-permute-done | bytes 32800 | tf_op jit(solution)/shard_map/ppermute | solution.py:100
  40.9 1.1 %collective-permute-done.13.refs_7_ = f32[2,32,128]{2,1,0:T(8,128)S(1)} collective-permute-done((f32[2,32,128]{2,1,0:T(8,128)S(1)}, f32[2,32,128]{2,1,0:T(8,128)S(1)}, u32[]{:S(2)}, u32[]{:S(2)}) %collective-permute-start.13) | collective-permute-done | bytes 32800 | tf_op jit(solution)/shard_map/ppermute | solution.py:100
  42.0 0.0 collective-permute-done.12.refs_6_
  42.0 1.0 %shard_map.106 = (f32[32,32,128]{2,1,0:T(8,128)S(1)}, f32[32,32,128]{2,1,0:T(8,128)S(1)}, f32[4,32,128]{2,1,0:T(8,128)S(1)}, f32[2,8,128]{2,1,0:T(8,128)S(1)}, f32[2,8,128]{2,1,0:T(8,128)S(1)}) custom-call(s32[3]{0:T(128)S(1)} %pad_add_fusion.where, f32[32,32,128]{2,1,0:T(8,128)S(1)} %get-tuple-element.77.refs_0_, ...), custom_call_target="tpu_custom_call" | custom-call | tf_op jit(solution)/shard_map/pallas_call | solution.py:25
  43.0 1.6 %collective-permute-start.15 = (f32[4,32,128]{2,1,0:T(8,128)S(1)}, f32[4,32,128]{2,1,0:T(8,128)S(1)}, u32[]{:S(2)}, u32[]{:S(2)}) collective-permute-start(f32[4,32,128]{2,1,0:T(8,128)S(1)} %get-tuple-element.83.refs_6_), channel_id=1, source_target_pairs={{0,16},{16,0},{1,17},{17,1},{2,18},{18,2},{3,19},{19,3},{4,20},{20... | collective-permute-start | bytes 196616 | tf_op jit(solution)/shard_map/ppermute | solution.py:92
  44.6 0.9 %collective-permute-start.16 = (f32[2,8,128]{2,1,0:T(8,128)S(1)}, f32[2,8,128]{2,1,0:T(8,128)S(1)}, u32[]{:S(2)}, u32[]{:S(2)}) collective-permute-start(f32[2,8,128]{2,1,0:T(8,128)S(1)} %get-tuple-element.84.refs_7_), channel_id=1, source_target_pairs={{0,4},{4,0},{8,12},{12,8},{1,5},{5,1},{9,13},{13,9},{2,6},{6,2},{1... | collective-permute-start | bytes 24584 | tf_op jit(solution)/shard_map/ppermute | solution.py:89
  45.5 2.9 %collective-permute-start.17 = (f32[2,8,128]{2,1,0:T(8,128)S(1)}, f32[2,8,128]{2,1,0:T(8,128)S(1)}, u32[]{:S(2)}, u32[]{:S(2)}) collective-permute-start(f32[2,8,128]{2,1,0:T(8,128)S(1)} %get-tuple-element.85.refs_8_), channel_id=1, source_target_pairs={{0,12},{4,8},{8,4},{12,0},{1,13},{5,9},{9,5},{13,1},{2,14},{6,10},... | collective-permute-start | bytes 24584 | tf_op jit(solution)/shard_map/ppermute | solution.py:88
  48.4 0.0 collective-permute-done.16.refs_10_
  48.4 2.5 %collective-permute-done.17.refs_11_ = f32[2,8,128]{2,1,0:T(8,128)S(1)} collective-permute-done((f32[2,8,128]{2,1,0:T(8,128)S(1)}, f32[2,8,128]{2,1,0:T(8,128)S(1)}, u32[]{:S(2)}, u32[]{:S(2)}) %collective-permute-start.17) | collective-permute-done | bytes 8224 | tf_op jit(solution)/shard_map/ppermute | solution.py:88
  51.0 2.2 %shard_map.107 = (f32[32,32,128]{2,1,0:T(8,128)}, f32[32,32,128]{2,1,0:T(8,128)}, f32[32,32,128]{2,1,0:T(8,128)S(1)}, f32[32,32,128]{2,1,0:T(8,128)S(1)}, f32[4,...) custom-call(s32[3]{0:T(128)S(1)} %pad_add_fusion.where, ...), custom_call_target="tpu_custom_call" | custom-call | tf_op jit(solution)/shard_map/pallas_call | solution.py:25
  53.1 1.6 %collective-permute-start.20 = (f32[2,32,128]{2,1,0:T(8,128)S(1)}, f32[2,32,128]{2,1,0:T(8,128)S(1)}, u32[]{:S(2)}, u32[]{:S(2)}) collective-permute-start(f32[2,32,128]{2,1,0:T(8,128)S(1)} %get-tuple-element.93), channel_id=1, source_target_pairs={{0,3},{1,2},{2,1},{3,0},{4,7},{5,6},{6,5},{7,4},{8,11},{9,10},{10,... | collective-permute-start | bytes 98312 | tf_op jit(solution)/shard_map/ppermute | solution.py:100
  54.8 0.5 collective-permute-start.19
  55.3 1.2 %collective-permute-done.20.refs_8_ = f32[2,32,128]{2,1,0:T(8,128)S(1)} collective-permute-done((f32[2,32,128]{2,1,0:T(8,128)S(1)}, f32[2,32,128]{2,1,0:T(8,128)S(1)}, u32[]{:S(2)}, u32[]{:S(2)}) %collective-permute-start.20) | collective-permute-done | bytes 32800 | tf_op jit(solution)/shard_map/ppermute | solution.py:100
  56.5 2.2 %collective-permute-done.19.refs_7_ = f32[2,32,128]{2,1,0:T(8,128)S(1)} collective-permute-done((f32[2,32,128]{2,1,0:T(8,128)S(1)}, f32[2,32,128]{2,1,0:T(8,128)S(1)}, u32[]{:S(2)}, u32[]{:S(2)}) %collective-permute-start.19) | collective-permute-done | bytes 32800 | tf_op jit(solution)/shard_map/ppermute | solution.py:100
  58.7 1.7 %shard_map.108 = (f32[32,32,128]{2,1,0:T(8,128)}, f32[32,32,128]{2,1,0:T(8,128)}) custom-call(s32[3]{0:T(128)S(1)} %pad_add_fusion.where, f32[32,32,128]{2,1,0:T(8,128)S(1)} %get-tuple-element.90.refs_0_, f32[32,32,128]{2,1,0:T(8,128)S(1)} %get-tuple-element.91.refs_1_, f32[32,32,128]{2,1,0:T(8,128)S(1)} %get-tuple-element.63.refs_2_, ...), custom_call_target="tpu_custom_call" | custom-call | tf_op jit(solution)/shard_map/pallas_call | solution.py:25
  (16 shorter events, 0.0 us)
Async XLA Ops:
  0.6 0.7 %copy-start.5 = (s32[32,128]{1,0:T(8,128)S(1)}, s32[32,128]{1,0:T(8,128)}, u32[]{:S(2)}) copy-start(s32[32,128]{1,0:T(8,128)} %refs_4_.1) | copy-start | bytes 49156
  0.6 0.7 %copy-start.6 = (s32[32,128]{1,0:T(8,128)S(1)}, s32[32,128]{1,0:T(8,128)}, u32[]{:S(2)}) copy-start(s32[32,128]{1,0:T(8,128)} %refs_5_.1) | copy-start | bytes 49156
  1.4 1.0 %copy-start = (f32[32,32,128]{2,1,0:T(8,128)S(1)}, f32[32,32,128]{2,1,0:T(8,128)}, u32[]{:S(2)}) copy-start(f32[32,32,128]{2,1,0:T(8,128)} %refs_0_.1) | copy-start | bytes 1572868
  2.4 1.0 %copy-start.1 = (f32[32,32,128]{2,1,0:T(8,128)S(1)}, f32[32,32,128]{2,1,0:T(8,128)}, u32[]{:S(2)}) copy-start(f32[32,32,128]{2,1,0:T(8,128)} %refs_1_.1) | copy-start | bytes 1572868
  3.5 1.0 %copy-start.2 = (f32[32,32,128]{2,1,0:T(8,128)S(1)}, f32[32,32,128]{2,1,0:T(8,128)}, u32[]{:S(2)}) copy-start(f32[32,32,128]{2,1,0:T(8,128)} %refs_2_.2) | copy-start | bytes 1572868
  4.5 1.0 %copy-start.3 = (f32[32,32,128]{2,1,0:T(8,128)S(1)}, f32[32,32,128]{2,1,0:T(8,128)}, u32[]{:S(2)}) copy-start(f32[32,32,128]{2,1,0:T(8,128)} %refs_3_.1) | copy-start | bytes 1572868
  5.5 15.6 %copy-start.4 = (f32[32,32,128]{2,1,0:T(8,128)S(1)}, f32[32,32,128]{2,1,0:T(8,128)}, u32[]{:S(2)}) copy-start(f32[32,32,128]{2,1,0:T(8,128)} %refs_2_.3) | copy-start | bytes 1572868
  7.1 14.1 %collective-permute-start = (f32[6,32,128]{2,1,0:T(8,128)S(1)}, f32[6,32,128]{2,1,0:T(8,128)S(1)}, u32[]{:S(2)}, u32[]{:S(2)}) collective-permute-start(f32[6,32,128]{2,1,0:T(8,128)S(1)} %get-tuple-element.55.refs_6_), channel_id=1, source_target_pairs={{0,16},{16,0},{1,17},{17,1},{2,18},{18,2},{3,19},{19,3},{4,20},{20... | collective-permute-start | bytes 294920 | tf_op jit(solution)/shard_map/ppermute | solution.py:92
  10.1 11.1 %collective-permute-start.5 = (f32[4,32,128]{2,1,0:T(8,128)S(1)}, f32[4,32,128]{2,1,0:T(8,128)S(1)}, u32[]{:S(2)}, u32[]{:S(2)}) collective-permute-start(f32[4,32,128]{2,1,0:T(8,128)S(1)} %get-tuple-element.58.refs_12_), channel_id=1, source_target_pairs={{0,3},{1,2},{2,1},{3,0},{4,7},{5,6},{6,5},{7,4},{8,11},{9,10},{10,... | collective-permute-start | bytes 196616 | tf_op jit(solution)/shard_map/ppermute | solution.py:100
  10.8 10.4 %collective-permute-start.4 = (f32[4,32,128]{2,1,0:T(8,128)S(1)}, f32[4,32,128]{2,1,0:T(8,128)S(1)}, u32[]{:S(2)}, u32[]{:S(2)}) collective-permute-start(f32[4,32,128]{2,1,0:T(8,128)S(1)} %get-tuple-element.58.refs_12_), channel_id=1, source_target_pairs={{0,2},{1,3},{2,0},{3,1},{4,6},{5,7},{6,4},{7,5},{8,10},{9,11},{10,... | collective-permute-start | bytes 196616 | tf_op jit(solution)/shard_map/ppermute | solution.py:100
  11.6 9.5 %collective-permute-start.3 = (f32[4,32,128]{2,1,0:T(8,128)S(1)}, f32[4,32,128]{2,1,0:T(8,128)S(1)}, u32[]{:S(2)}, u32[]{:S(2)}) collective-permute-start(f32[4,32,128]{2,1,0:T(8,128)S(1)} %get-tuple-element.58.refs_12_), channel_id=1, source_target_pairs={{0,1},{1,0},{2,3},{3,2},{4,5},{5,4},{6,7},{7,6},{8,9},{9,8},{10,11... | collective-permute-start | bytes 196616 | tf_op jit(solution)/shard_map/ppermute | solution.py:100
  12.0 3.7 %collective-permute-start.1 = (f32[3,8,128]{2,1,0:T(8,128)S(1)}, f32[3,8,128]{2,1,0:T(8,128)S(1)}, u32[]{:S(2)}, u32[]{:S(2)}) collective-permute-start(f32[3,8,128]{2,1,0:T(8,128)S(1)} %get-tuple-element.56.refs_7_), channel_id=1, source_target_pairs={{0,4},{4,0},{8,12},{12,8},{1,5},{5,1},{9,13},{13,9},{2,6},{6,2},{1... | collective-permute-start | bytes 36872 | tf_op jit(solution)/shard_map/ppermute | solution.py:89
  15.7 5.5 %collective-permute-start.2 = (f32[3,8,128]{2,1,0:T(8,128)S(1)}, f32[3,8,128]{2,1,0:T(8,128)S(1)}, u32[]{:S(2)}, u32[]{:S(2)}) collective-permute-start(f32[3,8,128]{2,1,0:T(8,128)S(1)} %get-tuple-element.57.refs_8_), channel_id=1, source_target_pairs={{0,12},{4,8},{8,4},{12,0},{1,13},{5,9},{9,5},{13,1},{2,14},{6,10},... | collective-permute-start | bytes 36872 | tf_op jit(solution)/shard_map/ppermute | solution.py:88
  23.4 5.6 %collective-permute-start.6 = (f32[4,32,128]{2,1,0:T(8,128)S(1)}, f32[4,32,128]{2,1,0:T(8,128)S(1)}, u32[]{:S(2)}, u32[]{:S(2)}) collective-permute-start(f32[4,32,128]{2,1,0:T(8,128)S(1)} %get-tuple-element.66.refs_5_), channel_id=1, source_target_pairs={{0,1},{1,0},{2,3},{3,2},{4,5},{5,4},{6,7},{7,6},{8,9},{9,8},{10,11... | collective-permute-start | bytes 196616 | tf_op jit(solution)/shard_map/ppermute | solution.py:100
  23.4 3.3 %collective-permute-start.8 = (f32[2,32,128]{2,1,0:T(8,128)S(1)}, f32[2,32,128]{2,1,0:T(8,128)S(1)}, u32[]{:S(2)}, u32[]{:S(2)}) collective-permute-start(f32[2,32,128]{2,1,0:T(8,128)S(1)} %get-tuple-element.67), channel_id=1, source_target_pairs={{0,3},{1,2},{2,1},{3,0},{4,7},{5,6},{6,5},{7,4},{8,11},{9,10},{10,... | collective-permute-start | bytes 98312 | tf_op jit(solution)/shard_map/ppermute | solution.py:100
  25.0 3.9 %collective-permute-start.7 = (f32[2,32,128]{2,1,0:T(8,128)S(1)}, f32[2,32,128]{2,1,0:T(8,128)S(1)}, u32[]{:S(2)}, u32[]{:S(2)}) collective-permute-start(f32[2,32,128]{2,1,0:T(8,128)S(1)} %get-tuple-element.67), channel_id=1, source_target_pairs={{0,2},{1,3},{2,0},{3,1},{4,6},{5,7},{6,4},{7,5},{8,10},{9,11},{10,... | collective-permute-start | bytes 98312 | tf_op jit(solution)/shard_map/ppermute | solution.py:100
  29.9 6.1 %collective-permute-start.9 = (f32[4,32,128]{2,1,0:T(8,128)S(1)}, f32[4,32,128]{2,1,0:T(8,128)S(1)}, u32[]{:S(2)}, u32[]{:S(2)}) collective-permute-start(f32[4,32,128]{2,1,0:T(8,128)S(1)} %get-tuple-element.70.refs_6_), channel_id=1, source_target_pairs={{0,16},{16,0},{1,17},{17,1},{2,18},{18,2},{3,19},{19,3},{4,20},{20... | collective-permute-start | bytes 196616 | tf_op jit(solution)/shard_map/ppermute | solution.py:92
  30.5 3.7 %collective-permute-start.10 = (f32[2,8,128]{2,1,0:T(8,128)S(1)}, f32[2,8,128]{2,1,0:T(8,128)S(1)}, u32[]{:S(2)}, u32[]{:S(2)}) collective-permute-start(f32[2,8,128]{2,1,0:T(8,128)S(1)} %get-tuple-element.71.refs_7_), channel_id=1, source_target_pairs={{0,4},{4,0},{8,12},{12,8},{1,5},{5,1},{9,13},{13,9},{2,6},{6,2},{1... | collective-permute-start | bytes 24584 | tf_op jit(solution)/shard_map/ppermute | solution.py:89
  30.5 5.4 %collective-permute-start.11 = (f32[2,8,128]{2,1,0:T(8,128)S(1)}, f32[2,8,128]{2,1,0:T(8,128)S(1)}, u32[]{:S(2)}, u32[]{:S(2)}) collective-permute-start(f32[2,8,128]{2,1,0:T(8,128)S(1)} %get-tuple-element.72.refs_8_), channel_id=1, source_target_pairs={{0,12},{4,8},{8,4},{12,0},{1,13},{5,9},{9,5},{13,1},{2,14},{6,10},... | collective-permute-start | bytes 24584 | tf_op jit(solution)/shard_map/ppermute | solution.py:88
  37.5 4.5 %collective-permute-start.12 = (f32[4,32,128]{2,1,0:T(8,128)S(1)}, f32[4,32,128]{2,1,0:T(8,128)S(1)}, u32[]{:S(2)}, u32[]{:S(2)}) collective-permute-start(f32[4,32,128]{2,1,0:T(8,128)S(1)} %get-tuple-element.79.refs_5_), channel_id=1, source_target_pairs={{0,1},{1,0},{2,3},{3,2},{4,5},{5,4},{6,7},{7,6},{8,9},{9,8},{10,11... | collective-permute-start | bytes 196616 | tf_op jit(solution)/shard_map/ppermute | solution.py:100
  37.5 3.4 %collective-permute-start.14 = (f32[2,32,128]{2,1,0:T(8,128)S(1)}, f32[2,32,128]{2,1,0:T(8,128)S(1)}, u32[]{:S(2)}, u32[]{:S(2)}) collective-permute-start(f32[2,32,128]{2,1,0:T(8,128)S(1)} %get-tuple-element.80), channel_id=1, source_target_pairs={{0,3},{1,2},{2,1},{3,0},{4,7},{5,6},{6,5},{7,4},{8,11},{9,10},{10,... | collective-permute-start | bytes 98312 | tf_op jit(solution)/shard_map/ppermute | solution.py:100
  38.0 4.0 %collective-permute-start.13 = (f32[2,32,128]{2,1,0:T(8,128)S(1)}, f32[2,32,128]{2,1,0:T(8,128)S(1)}, u32[]{:S(2)}, u32[]{:S(2)}) collective-permute-start(f32[2,32,128]{2,1,0:T(8,128)S(1)} %get-tuple-element.80), channel_id=1, source_target_pairs={{0,2},{1,3},{2,0},{3,1},{4,6},{5,7},{6,4},{7,5},{8,10},{9,11},{10,... | collective-permute-start | bytes 98312 | tf_op jit(solution)/shard_map/ppermute | solution.py:100
  43.0 8.0 %collective-permute-start.15 = (f32[4,32,128]{2,1,0:T(8,128)S(1)}, f32[4,32,128]{2,1,0:T(8,128)S(1)}, u32[]{:S(2)}, u32[]{:S(2)}) collective-permute-start(f32[4,32,128]{2,1,0:T(8,128)S(1)} %get-tuple-element.83.refs_6_), channel_id=1, source_target_pairs={{0,16},{16,0},{1,17},{17,1},{2,18},{18,2},{3,19},{19,3},{4,20},{20... | collective-permute-start | bytes 196616 | tf_op jit(solution)/shard_map/ppermute | solution.py:92
  44.6 3.8 %collective-permute-start.16 = (f32[2,8,128]{2,1,0:T(8,128)S(1)}, f32[2,8,128]{2,1,0:T(8,128)S(1)}, u32[]{:S(2)}, u32[]{:S(2)}) collective-permute-start(f32[2,8,128]{2,1,0:T(8,128)S(1)} %get-tuple-element.84.refs_7_), channel_id=1, source_target_pairs={{0,4},{4,0},{8,12},{12,8},{1,5},{5,1},{9,13},{13,9},{2,6},{6,2},{1... | collective-permute-start | bytes 24584 | tf_op jit(solution)/shard_map/ppermute | solution.py:89
  45.5 5.4 %collective-permute-start.17 = (f32[2,8,128]{2,1,0:T(8,128)S(1)}, f32[2,8,128]{2,1,0:T(8,128)S(1)}, u32[]{:S(2)}, u32[]{:S(2)}) collective-permute-start(f32[2,8,128]{2,1,0:T(8,128)S(1)} %get-tuple-element.85.refs_8_), channel_id=1, source_target_pairs={{0,12},{4,8},{8,4},{12,0},{1,13},{5,9},{9,5},{13,1},{2,14},{6,10},... | collective-permute-start | bytes 24584 | tf_op jit(solution)/shard_map/ppermute | solution.py:88
  53.1 5.5 %collective-permute-start.18 = (f32[4,32,128]{2,1,0:T(8,128)S(1)}, f32[4,32,128]{2,1,0:T(8,128)S(1)}, u32[]{:S(2)}, u32[]{:S(2)}) collective-permute-start(f32[4,32,128]{2,1,0:T(8,128)S(1)} %get-tuple-element.92.refs_5_), channel_id=1, source_target_pairs={{0,1},{1,0},{2,3},{3,2},{4,5},{5,4},{6,7},{7,6},{8,9},{9,8},{10,11... | collective-permute-start | bytes 196616 | tf_op jit(solution)/shard_map/ppermute | solution.py:100
  53.1 3.3 %collective-permute-start.20 = (f32[2,32,128]{2,1,0:T(8,128)S(1)}, f32[2,32,128]{2,1,0:T(8,128)S(1)}, u32[]{:S(2)}, u32[]{:S(2)}) collective-permute-start(f32[2,32,128]{2,1,0:T(8,128)S(1)} %get-tuple-element.93), channel_id=1, source_target_pairs={{0,3},{1,2},{2,1},{3,0},{4,7},{5,6},{6,5},{7,4},{8,11},{9,10},{10,... | collective-permute-start | bytes 98312 | tf_op jit(solution)/shard_map/ppermute | solution.py:100
  54.8 3.9 %collective-permute-start.19 = (f32[2,32,128]{2,1,0:T(8,128)S(1)}, f32[2,32,128]{2,1,0:T(8,128)S(1)}, u32[]{:S(2)}, u32[]{:S(2)}) collective-permute-start(f32[2,32,128]{2,1,0:T(8,128)S(1)} %get-tuple-element.93), channel_id=1, source_target_pairs={{0,2},{1,3},{2,0},{3,1},{4,6},{5,7},{6,4},{7,5},{8,10},{9,11},{10,... | collective-permute-start | bytes 98312 | tf_op jit(solution)/shard_map/ppermute | solution.py:100
